TPU v7x, 128 devices: a whole 4x4x4 slice. The times are simulated.
128 devices in a mesh: chan: 8 (over y, x_hi), strip: 16 (over z, x_lo, core).
Axes of the slice: x: 4 (x_hi: 2, x_lo: 2; x = x_hi * 2 + x_lo), y: 4, z: 4, core: 2. Of those that a mesh axis runs over, the one named last changes fastest.
Arguments:
- wave_field: float32 [2, 16, 1536, 1536], P(None, 'chan', 'strip'), may hold values from -6 to 6
- radial_op: float32 [1536, 1536], replicated, may hold values from -1 to 1, as said below
- coupling: float32 [2, 16, 8], replicated, may hold values from -4 to 4
- couple: int32 [16, 8], replicated, may hold values from 0 to 15
- partner: int32 [16], replicated, may hold values from 0 to 15, as said below
- extent: int32 [16], replicated, may hold values from 384 to 1536, as said below
Outputs:
- first_step: float32 [2, 16, 1536, 1536], P(None, None, 'strip', 'chan')
- second_step: float32 [2, 16, 1536, 1536], P(None, None, 'strip', 'chan')
Inputs may be any that keep to these rules, and one draw needn't show every extreme that they name: radial_op is symmetric. partner pairs the channels: partner(partner(c)) == c and partner(c) != c. Each extent is a multiple of 96; some channel has extent 1536 and some 1536 // 4.
All inputs are finite; a program needn't handle non-finite values.
Results may differ from a plain program's by a relative error of at most 0.0003.
Values sent between devices are 32-bit elements; how exact they have to be, the bound alone decides.
No kernel may reach another device: no remote copies, remote signals or barrier semaphores. Data moves between devices by JAX's collectives and lax.ppermute only.
A program may use at most 128 MiB of HBM per device.

v0:
```python
import jax
import jax.numpy as jnp
from jax import lax
from jax.sharding import PartitionSpec as P


def potentials(row_pos, col_pos, count, orders):
    spacing = 8.0 / count
    first = row_pos.astype(jnp.float32) * spacing
    second = col_pos.astype(jnp.float32) * spacing
    lesser = jnp.minimum(first[:, None], second[None, :])
    greater = jnp.maximum(first[:, None], second[None, :])
    root = jnp.sqrt(greater * greater + 1.0)
    result = []
    for order in range(orders):
        result.append(lesser**order / root ** (order + 1))
    return result


def couple_terms(field, image_rows, mirrored, coupling, couple, partner, pots, live):
    total = image_rows + jnp.take(mirrored, partner, axis=1)
    real_part = total[0]
    imag_part = total[1]
    for order in range(len(pots)):
        source = jnp.take(field, couple[:, order], axis=1)
        c_real = coupling[0, :, order][:, None, None]
        c_imag = coupling[1, :, order][:, None, None]
        real_part = real_part + pots[order] * (c_real * source[0] - c_imag * source[1])
        imag_part = imag_part + pots[order] * (c_real * source[1] + c_imag * source[0])
    return jnp.where(live[None], jnp.stack([real_part, imag_part]), 0.0)


def radial_product(radial_op, block):
    return jnp.einsum("ak,pckb->pcab", radial_op, block, precision=lax.Precision.HIGHEST)


def local(wave_field, radial_op, coupling, couple, partner, extent):
    chans = lax.axis_size("chan")
    grid = wave_field.shape[3]
    strip_rows = wave_field.shape[2]
    chan_cols = grid // chans
    row_pos = lax.axis_index("strip") * strip_rows + jnp.arange(strip_rows)
    col_pos = lax.axis_index("chan") * chan_cols + jnp.arange(chan_cols)
    pots = potentials(row_pos, col_pos, grid, coupling.shape[2])
    live = (row_pos[None, :, None] < extent[:, None, None]) & (
        col_pos[None, None, :] < extent[:, None, None]
    )

    def radial(block):
        return radial_product(radial_op, block)

    def product_columns(field_rows):
        return radial(lax.all_to_all(field_rows, "strip", split_axis=3, concat_axis=2, tiled=True))

    def both_terms(image):
        image_rows = lax.all_to_all(image, "strip", split_axis=2, concat_axis=3, tiled=True)
        return (image_rows, jnp.swapaxes(image, 2, 3))

    image_rows, mirrored = both_terms(product_columns(wave_field))
    field_tiles, rows_tiles, mirror_tiles = (
        lax.all_to_all(wave_field, "chan", split_axis=3, concat_axis=1, tiled=True),
        lax.all_to_all(image_rows, "chan", split_axis=3, concat_axis=1, tiled=True),
        lax.all_to_all(mirrored, "chan", split_axis=3, concat_axis=1, tiled=True),
    )
    first_step = couple_terms(
        field_tiles, rows_tiles, mirror_tiles, coupling, couple, partner, pots, live
    )
    image = product_columns(
        lax.all_to_all(first_step, "chan", split_axis=1, concat_axis=3, tiled=True)
    )
    image_rows, mirrored = both_terms(image)
    rows_tiles = lax.all_to_all(image_rows, "chan", split_axis=3, concat_axis=1, tiled=True)
    mirror_tiles = lax.all_to_all(mirrored, "chan", split_axis=3, concat_axis=1, tiled=True)
    applied = couple_terms(
        first_step, rows_tiles, mirror_tiles, coupling, couple, partner, pots, live
    )
    second_step = 2.0 * applied - field_tiles
    return (first_step, second_step)


def solution(mesh):
    placed = (P(None, "chan", "strip", None), P(), P(), P(), P(), P())
    return jax.shard_map(
        local,
        mesh=mesh,
        in_specs=placed,
        out_specs=(P(None, None, "strip", "chan"), P(None, None, "strip", "chan")),
        check_vma=False,
    )
```

profile of v0, /device:TPU:1, one launch (start us, length us, event | category | flops | bytes accessed | tf_op | source)
XLA Modules:
  0.0 539.2 jit_solution(1031127415181671405)
XLA Ops:
  0.6 5.5 %copy.82 = f32[2,2,96,1536]{2,1,0,3:T(2,128)} copy(f32[2,2,96,1536]{3,2,1,0:T(8,128)} %param.8) | data formatting | bytes 4718592 | tf_op args[0]
  6.1 45.6 %all_to_all.180 = f32[2,2,96,1536]{2,1,0,3:T(2,128)S(1)} all-to-all(f32[2,2,96,1536]{2,1,0,3:T(2,128)} %copy.82), channel_id=1, replica_groups=mesh['chan'=8,'strip'=16] {'strip'}, dimensions={3} | all-to-all | bytes 4718592 | tf_op jit(solution)/shard_map/all_to_all | solution.py:53
  51.7 6.4 %all-to-all-start.4 = ((f32[2,2,96,1536]{2,1,0,3:T(2,128)}), f32[2,2,96,1536]{2,1,0,3:T(2,128)}, u32[]{:S(2)}, u32[]{:S(2)}) async-start(f32[2,2,96,1536]{2,1,0,3:T(2,128)} %copy.82), calls=%async_computation.4 | async-start | bytes 6291456 | tf_op jit(solution)/shard_map/all_to_all | solution.py:61
  66.0 15.1 %fusion.2 = f32[2,2,96,1536]{3,2,1,0:T(8,128)S(1)} fusion(f32[2,2,1536,96]{2,3,1,0:T(8,128)} %all_to_all.133, f32[1536,1536]{1,0:T(8,128)} %param.9), kind=kOutput, calls=%fused_computation.20 | convolution fusion | flops 10871635968 | bytes 14155776 | tf_op jit(solution)/shard_map/ak,pckb->pcab/dot_general | solution.py:34
  84.4 12.1 %all-to-all-done.4 = f32[2,2,96,1536]{2,1,0,3:T(2,128)} async-done(((f32[2,2,96,1536]{2,1,0,3:T(2,128)}), f32[2,2,96,1536]{2,1,0,3:T(2,128)}, u32[]{:S(2)}, u32[]{:S(2)}) %all-to-all-start.4) | async-done | bytes 2359328 | tf_op jit(solution)/shard_map/all_to_all | solution.py:61
  96.5 6.6 %all-to-all-start.1 = ((f32[2,2,1536,96]{3,1,0,2:T(2,128)}), f32[2,2,1536,96]{3,1,0,2:T(2,128)}, u32[]{:S(2)}, u32[]{:S(2)}) async-start(f32[2,2,1536,96]{3,1,0,2:T(2,128)} %copy.84), calls=%async_computation.1 | async-start | bytes 6291456 | tf_op jit(solution)/shard_map/all_to_all | solution.py:56
  112.5 29.2 %all-to-all-done.1 = f32[2,2,1536,96]{3,1,0,2:T(2,128)} async-done(((f32[2,2,1536,96]{3,1,0,2:T(2,128)}), f32[2,2,1536,96]{3,1,0,2:T(2,128)}, u32[]{:S(2)}, u32[]{:S(2)}) %all-to-all-start.1) | async-done | bytes 2359328 | tf_op jit(solution)/shard_map/all_to_all | solution.py:56
  141.7 4.9 all-to-all-start.3
  149.3 4.5 copy.94
  167.7 5.4 copy.131
  173.1 4.6 copy.110
  177.7 7.7 %all-to-all-done.3 = f32[2,2,96,1536]{2,1,0,3:T(2,128)} async-done(((f32[2,2,96,1536]{2,1,0,3:T(2,128)}), f32[2,2,96,1536]{2,1,0,3:T(2,128)}, u32[]{:S(2)}, u32[]{:S(2)}) %all-to-all-start.3) | async-done | bytes 2359328 | tf_op jit(solution)/shard_map/all_to_all | solution.py:63
  220.8 5.8 %copy.115 = f32[2,2,96,8,192]{4,2,1,3,0:T(8,128)} copy(f32[2,2,96,8,192]{2,1,0,4,3:T(2,128)} %bitcast.13) | data formatting | bytes 4718592 | tf_op jit(solution)/shard_map/all_to_all | solution.py:63
  226.6 4.5 gather_fusion
  231.1 5.9 %copy.113 = f32[2,2,96,8,192]{4,2,0,1,3:T(8,128)} copy(f32[2,2,96,8,192]{2,1,0,4,3:T(2,128)} %bitcast.8) | data formatting | bytes 4718592 | tf_op jit(solution)/shard_map/all_to_all | solution.py:62
  242.8 7.3 %fusion.26 = f32[1,16,96,192]{3,2,0,1:T(8,128)S(1)} fusion(f32[2,16,96,192]{3,2,0,1:T(8,128)S(1)} %bitcast_add_fusion.1, f32[2,16,96,192]{3,2,0,1:T(8,128)S(1)} %copy-done.9, f32[2,16,96,192]{3,2,0,1:T(8,128)S(1)} %copy-done.10, f32[2,16,96,192]{3,2,0,1:T(8,128)S(1)} %copy-done.11, f32[2,16,96,192]{3,2,0,1:T(8,128)S(1)} %select_bitcast_fusion.11, ...), kind=kLoop, calls=%fused_computation.71 | loop fusion | flops 11796480 | bytes 21824512 | tf_op jit(solution)/shard_map/add | solution.py:29
  256.2 43.8 %all_to_all.181 = f32[2,16,96,192]{3,2,0,1:T(8,128)} all-to-all(f32[2,16,96,192]{3,2,0,1:T(8,128)S(1)} %maximum_select_fusion), channel_id=1, replica_groups=mesh['chan'=8,'strip'=16] {'chan'}, dimensions={1} | all-to-all | bytes 4718592 | tf_op jit(solution)/shard_map/all_to_all | solution.py:69
  300.0 5.9 %copy.116 = f32[2,2,96,8,192]{2,1,0,4,3:T(2,128)} copy(f32[2,2,96,8,192]{4,2,0,1,3:T(8,128)} %bitcast.180) | data formatting | bytes 4718592 | tf_op jit(solution)/shard_map/all_to_all | solution.py:69
  305.9 45.1 %all_to_all.182 = f32[2,2,96,1536]{2,1,0,3:T(2,128)S(1)} all-to-all(f32[2,2,96,1536]{2,1,0,3:T(2,128)} %bitcast.177), channel_id=1, replica_groups=mesh['chan'=8,'strip'=16] {'strip'}, dimensions={3} | all-to-all | bytes 4718592 | tf_op jit(solution)/shard_map/all_to_all | solution.py:53
  358.8 16.1 %fusion = f32[2,2,96,1536]{3,2,1,0:T(8,128)} fusion(f32[2,2,1536,96]{2,3,1,0:T(8,128)} %all_to_all.157, f32[1536,1536]{1,0:T(8,128)} %param.9), kind=kOutput, calls=%fused_computation.18 | convolution fusion | flops 10871635968 | bytes 14155776 | tf_op jit(solution)/shard_map/ak,pckb->pcab/dot_general | solution.py:34
  374.9 5.5 %copy.99 = f32[2,2,1536,96]{3,1,0,2:T(2,128)} copy(f32[2,2,1536,96]{2,3,1,0:T(8,128)} %bitcast.171) | data formatting | bytes 4718592 | tf_op jit(solution)/shard_map/ak,pckb->pcab/transpose | solution.py:34
  380.4 5.4 all-to-all-start.7
  385.8 5.5 %copy.104 = f32[2,2,96,1536]{2,1,0,3:T(2,128)} copy(f32[2,2,96,1536]{3,2,1,0:T(8,128)} %fusion) | data formatting | bytes 4718592 | tf_op jit(solution)/shard_map/ak,pckb->pcab/dot_general | solution.py:34
  391.3 33.0 %all-to-all-done.7 = f32[2,2,1536,96]{3,1,0,2:T(2,128)} async-done(((f32[2,2,1536,96]{3,1,0,2:T(2,128)}), f32[2,2,1536,96]{3,1,0,2:T(2,128)}, u32[]{:S(2)}, u32[]{:S(2)}) %all-to-all-start.7) | async-done | bytes 2359328 | tf_op jit(solution)/shard_map/all_to_all | solution.py:56
  424.3 4.7 all-to-all-start.9
  457.8 10.1 %all-to-all-done.9 = f32[2,2,96,1536]{2,1,0,3:T(2,128)} async-done(((f32[2,2,96,1536]{2,1,0,3:T(2,128)}), f32[2,2,96,1536]{2,1,0,3:T(2,128)}, u32[]{:S(2)}, u32[]{:S(2)}) %all-to-all-start.9) | async-done | bytes 2359328 | tf_op jit(solution)/shard_map/all_to_all | solution.py:73
  472.4 5.6 %select_bitcast_fusion = (f32[2,16,96,192]{3,2,0,1:T(8,128)S(1)}, f32[2,16,96,192]{3,2,0,1:T(8,128)}) fusion(f32[16,2,96,192]{3,2,1,0:T(8,128)} %gather_fusion.17, pred[16]{0:T(512)(128)(4,1)} %get-tuple-element.57, f32[16,2,96,192]{3,2,1,0:T(8,128)} %gather_fusion.16, pred[16]{0:T(512)(128)(4,1)} %get-tuple-element.59), kind=kLoop, calls=%fused_computation.32 | loop fusion | flops 1179648 | bytes 9437216 | tf_op jit(solution)/shard_map/jit(_take)/select_n | solution.py:25
  491.5 5.8 %copy.123 = f32[2,2,96,8,192]{4,2,1,3,0:T(8,128)} copy(f32[2,2,96,8,192]{2,1,0,4,3:T(2,128)} %bitcast.69) | data formatting | bytes 4718592 | tf_op jit(solution)/shard_map/all_to_all | solution.py:73
  501.8 8.5 %all-to-all-done.8 = f32[2,2,96,1536]{2,1,0,3:T(2,128)} async-done(((f32[2,2,96,1536]{2,1,0,3:T(2,128)}), f32[2,2,96,1536]{2,1,0,3:T(2,128)}, u32[]{:S(2)}, u32[]{:S(2)}) %all-to-all-start.8) | async-done | bytes 2359328 | tf_op jit(solution)/shard_map/all_to_all | solution.py:72
  510.2 5.9 %copy.121 = f32[2,2,96,8,192]{4,2,0,1,3:T(8,128)} copy(f32[2,2,96,8,192]{2,1,0,4,3:T(2,128)} %bitcast.65) | data formatting | bytes 4718592 | tf_op jit(solution)/shard_map/all_to_all | solution.py:72
  521.9 7.3 %fusion.12 = f32[1,16,96,192]{3,2,0,1:T(8,128)S(1)} fusion(f32[2,16,96,192]{3,2,0,1:T(8,128)S(1)} %bitcast_add_fusion, f32[2,16,96,192]{3,2,0,1:T(8,128)S(1)} %get-tuple-element.69, f32[2,16,96,192]{3,2,0,1:T(8,128)S(1)} %copy-done.2, f32[2,16,96,192]{3,2,0,1:T(8,128)S(1)} %copy-done.3, f32[2,16,96,192]{3,2,0,1:T(8,128)S(1)} %copy-done.4, ...), kind=kLoop, calls=%fused_computation.55 | loop fusion | flops 11796480 | bytes 21824512 | tf_op jit(solution)/shard_map/add | solution.py:29
  530.5 5.6 %fusion.19 = f32[1,16,96,192]{3,2,0,1:T(8,128)S(1)} fusion(f32[2,16,96,192]{3,2,0,1:T(8,128)S(1)} %bitcast_add_fusion, f32[2,16,96,192]{3,2,0,1:T(8,128)S(1)} %get-tuple-element.69, f32[2,16,96,192]{3,2,0,1:T(8,128)S(1)} %copy-done.2, f32[2,16,96,192]{3,2,0,1:T(8,128)S(1)} %copy-done.3, f32[2,16,96,192]{3,2,0,1:T(8,128)S(1)} %copy-done.4, ...), kind=kLoop, calls=%fused_computation.63 | loop fusion | flops 11796480 | bytes 21824512 | tf_op jit(solution)/shard_map/add | solution.py:28
  (219 shorter events, 152.7 us)
Async XLA Ops:
  51.7 44.7 %all-to-all-start.4 = ((f32[2,2,96,1536]{2,1,0,3:T(2,128)}), f32[2,2,96,1536]{2,1,0,3:T(2,128)}, u32[]{:S(2)}, u32[]{:S(2)}) async-start(f32[2,2,96,1536]{2,1,0,3:T(2,128)} %copy.82), calls=%async_computation.4 | async-start | bytes 6291456 | tf_op jit(solution)/shard_map/all_to_all | solution.py:61
  84.3 18.8 %copy-start.75 = (s32[16]{0:T(128)S(1)}, s32[16]{0:T(128)}, u32[]{:S(2)}) copy-start(s32[16]{0:T(128)} %param.12) | copy-start | bytes 196
  84.4 19.4 %copy-start.73 = (s32[16,8]{0,1:T(8,128)S(1)}, s32[16,8]{0,1:T(8,128)}, u32[]{:S(2)}) copy-start(s32[16,8]{0,1:T(8,128)} %param.11) | copy-start | bytes 1540
  96.5 45.2 %all-to-all-start.1 = ((f32[2,2,1536,96]{3,1,0,2:T(2,128)}), f32[2,2,1536,96]{3,1,0,2:T(2,128)}, u32[]{:S(2)}, u32[]{:S(2)}) async-start(f32[2,2,1536,96]{3,1,0,2:T(2,128)} %copy.84), calls=%async_computation.1 | async-start | bytes 6291456 | tf_op jit(solution)/shard_map/all_to_all | solution.py:56
  112.5 34.7 %copy-start.74 = (s32[16]{0:T(128)S(1)}, s32[16]{0:T(128)}, u32[]{:S(2)}) copy-start(s32[16]{0:T(128)} %param.13) | copy-start | bytes 196
  112.5 34.9 %copy-start.61 = (f32[2,16,8]{1,2,0:T(8,128)S(1)}, f32[2,16,8]{1,2,0:T(8,128)}, u32[]{:S(2)}) copy-start(f32[2,16,8]{1,2,0:T(8,128)} %param.10) | copy-start | bytes 3076
  141.7 43.8 %all-to-all-start.3 = ((f32[2,2,96,1536]{2,1,0,3:T(2,128)}), f32[2,2,96,1536]{2,1,0,3:T(2,128)}, u32[]{:S(2)}, u32[]{:S(2)}) async-start(f32[2,2,96,1536]{2,1,0,3:T(2,128)} %copy.89), calls=%async_computation.3 | async-start | bytes 6291456 | tf_op jit(solution)/shard_map/all_to_all | solution.py:63
  153.8 50.5 %copy-start = (f32[2,2,96,8,192]{4,2,0,1,3:T(8,128)}, f32[2,2,96,8,192]{4,2,0,1,3:T(8,128)S(1)}, u32[]{:S(2)}) copy-start(f32[2,2,96,8,192]{4,2,0,1,3:T(8,128)S(1)} %copy.94) | copy-start | bytes 7077892
  185.4 45.6 %all-to-all-start.2 = ((f32[2,2,96,1536]{2,1,0,3:T(2,128)}), f32[2,2,96,1536]{2,1,0,3:T(2,128)}, u32[]{:S(2)}, u32[]{:S(2)}) async-start(f32[2,2,96,1536]{2,1,0,3:T(2,128)} %bitcast.172), calls=%async_computation.2 | async-start | bytes 6291456 | tf_op jit(solution)/shard_map/all_to_all | solution.py:62
  237.0 5.6 %copy-start.37 = (f32[16]{0:T(128)S(1)}, f32[16]{0:T(128)}, u32[]{:S(2)}) copy-start(f32[16]{0:T(128)} %get-tuple-element.35) | copy-start | bytes 196
  242.7 7.4 %copy-start.12 = (f32[2,16,96,192]{3,2,0,1:T(8,128)S(1)}, f32[2,16,96,192]{3,2,0,1:T(8,128)}, u32[]{:S(2)}) copy-start(f32[2,16,96,192]{3,2,0,1:T(8,128)} %select_bitcast_fusion.12) | copy-start | bytes 7077892
  242.7 7.4 %copy-start.13 = (f32[2,16,96,192]{3,2,0,1:T(8,128)S(1)}, f32[2,16,96,192]{3,2,0,1:T(8,128)}, u32[]{:S(2)}) copy-start(f32[2,16,96,192]{3,2,0,1:T(8,128)} %select_bitcast_fusion.13) | copy-start | bytes 7077892
  242.7 7.7 %copy-start.14 = (f32[2,16,96,192]{3,2,0,1:T(8,128)S(1)}, f32[2,16,96,192]{3,2,0,1:T(8,128)}, u32[]{:S(2)}) copy-start(f32[2,16,96,192]{3,2,0,1:T(8,128)} %select_bitcast_fusion.14) | copy-start | bytes 7077892
  242.7 8.6 %copy-start.15 = (f32[2,16,96,192]{3,2,0,1:T(8,128)S(1)}, f32[2,16,96,192]{3,2,0,1:T(8,128)}, u32[]{:S(2)}) copy-start(f32[2,16,96,192]{3,2,0,1:T(8,128)} %select_bitcast_fusion.15) | copy-start | bytes 7077892
  242.7 8.6 %copy-start.27 = (f32[96,192]{1,0:T(8,128)S(1)}, f32[96,192]{1,0:T(8,128)}, u32[]{:S(2)}) copy-start(f32[96,192]{1,0:T(8,128)} %get-tuple-element.61) | copy-start | bytes 221188
  242.8 8.6 %copy-start.29 = (f32[96,192]{1,0:T(8,128)S(1)}, f32[96,192]{1,0:T(8,128)}, u32[]{:S(2)}) copy-start(f32[96,192]{1,0:T(8,128)} %get-tuple-element.62) | copy-start | bytes 221188
  242.8 8.6 %copy-start.31 = (f32[96,192]{1,0:T(8,128)S(1)}, f32[96,192]{1,0:T(8,128)}, u32[]{:S(2)}) copy-start(f32[96,192]{1,0:T(8,128)} %get-tuple-element.63) | copy-start | bytes 221188
  242.8 8.6 %copy-start.32 = (f32[96,192]{1,0:T(8,128)S(1)}, f32[96,192]{1,0:T(8,128)}, u32[]{:S(2)}) copy-start(f32[96,192]{1,0:T(8,128)} %get-tuple-element.64) | copy-start | bytes 221188
  242.8 8.6 %copy-start.33 = (f32[96,192]{1,0:T(8,128)S(1)}, f32[96,192]{1,0:T(8,128)}, u32[]{:S(2)}) copy-start(f32[96,192]{1,0:T(8,128)} %get-tuple-element.65) | copy-start | bytes 221188
  242.8 8.6 %copy-start.34 = (f32[96,192]{1,0:T(8,128)S(1)}, f32[96,192]{1,0:T(8,128)}, u32[]{:S(2)}) copy-start(f32[96,192]{1,0:T(8,128)} %get-tuple-element.66) | copy-start | bytes 221188
  242.8 8.6 %copy-start.35 = (f32[96,192]{1,0:T(8,128)S(1)}, f32[96,192]{1,0:T(8,128)}, u32[]{:S(2)}) copy-start(f32[96,192]{1,0:T(8,128)} %get-tuple-element.67) | copy-start | bytes 221188
  242.8 8.6 %copy-start.36 = (f32[96,192]{1,0:T(8,128)S(1)}, f32[96,192]{1,0:T(8,128)}, u32[]{:S(2)}) copy-start(f32[96,192]{1,0:T(8,128)} %get-tuple-element.68) | copy-start | bytes 221188
  380.4 43.9 %all-to-all-start.7 = ((f32[2,2,1536,96]{3,1,0,2:T(2,128)}), f32[2,2,1536,96]{3,1,0,2:T(2,128)}, u32[]{:S(2)}, u32[]{:S(2)}) async-start(f32[2,2,1536,96]{3,1,0,2:T(2,128)} %copy.99), calls=%async_computation.7 | async-start | bytes 6291456 | tf_op jit(solution)/shard_map/all_to_all | solution.py:56
  424.3 43.5 %all-to-all-start.9 = ((f32[2,2,96,1536]{2,1,0,3:T(2,128)}), f32[2,2,96,1536]{2,1,0,3:T(2,128)}, u32[]{:S(2)}, u32[]{:S(2)}) async-start(f32[2,2,96,1536]{2,1,0,3:T(2,128)} %copy.104), calls=%async_computation.9 | async-start | bytes 6291456 | tf_op jit(solution)/shard_map/all_to_all | solution.py:73
  467.9 42.4 %all-to-all-start.8 = ((f32[2,2,96,1536]{2,1,0,3:T(2,128)}), f32[2,2,96,1536]{2,1,0,3:T(2,128)}, u32[]{:S(2)}, u32[]{:S(2)}) async-start(f32[2,2,96,1536]{2,1,0,3:T(2,128)} %bitcast.64), calls=%async_computation.8 | async-start | bytes 6291456 | tf_op jit(solution)/shard_map/all_to_all | solution.py:72
  521.9 7.4 %copy-start.5 = (f32[2,16,96,192]{3,2,0,1:T(8,128)S(1)}, f32[2,16,96,192]{3,2,0,1:T(8,128)}, u32[]{:S(2)}) copy-start(f32[2,16,96,192]{3,2,0,1:T(8,128)} %get-tuple-element.73) | copy-start | bytes 7077892
  521.9 7.4 %copy-start.6 = (f32[2,16,96,192]{3,2,0,1:T(8,128)S(1)}, f32[2,16,96,192]{3,2,0,1:T(8,128)}, u32[]{:S(2)}) copy-start(f32[2,16,96,192]{3,2,0,1:T(8,128)} %get-tuple-element.74) | copy-start | bytes 7077892
  521.9 7.7 %copy-start.7 = (f32[2,16,96,192]{3,2,0,1:T(8,128)S(1)}, f32[2,16,96,192]{3,2,0,1:T(8,128)}, u32[]{:S(2)}) copy-start(f32[2,16,96,192]{3,2,0,1:T(8,128)} %get-tuple-element.75) | copy-start | bytes 7077892
  521.9 8.6 %copy-start.8 = (f32[2,16,96,192]{3,2,0,1:T(8,128)S(1)}, f32[2,16,96,192]{3,2,0,1:T(8,128)}, u32[]{:S(2)}) copy-start(f32[2,16,96,192]{3,2,0,1:T(8,128)} %get-tuple-element.76) | copy-start | bytes 7077892
  521.9 8.6 %copy-start.28 = (f32[96,192]{1,0:T(8,128)S(1)}, f32[96,192]{1,0:T(8,128)}, u32[]{:S(2)}) copy-start(f32[96,192]{1,0:T(8,128)} %get-tuple-element.61) | copy-start | bytes 221188
  521.9 8.6 %copy-start.30 = (f32[96,192]{1,0:T(8,128)S(1)}, f32[96,192]{1,0:T(8,128)}, u32[]{:S(2)}) copy-start(f32[96,192]{1,0:T(8,128)} %get-tuple-element.62) | copy-start | bytes 221188
  530.5 5.7 %copy-start.1 = (f32[2,2,96,8,192]{4,2,0,1,3:T(8,128)S(1)}, f32[2,2,96,8,192]{4,2,0,1,3:T(8,128)}, u32[]{:S(2)}) copy-start(f32[2,2,96,8,192]{4,2,0,1,3:T(8,128)} %copy-done) | copy-start | bytes 7077892
  (51 other events, 249.5 us)
where the time goes:
time: 550 us; the launch traced here: 539 us
  local copies, waits for them, and re-layouts  155 us (28%)
  blocking collectives  134 us (24%)
  waiting for transfers between devices  101 us (18%)
  other arithmetic  79.5 us (14%)
  starting transfers between devices  36.9 us (7%)
  matrix products  31.2 us (6%)
    all_to_all x2, blocking collectives, product_columns(): lax.all_to_all(field_rows, 'strip', split_axis=3, concat_axis=2, tiled=True)  90.7 us
    all_to_all x2, waiting for transfers between devices, both_terms(): lax.all_to_all(image, 'strip', split_axis=2, concat_axis=3, tiled=True)  62.2 us
    all_to_all x1, blocking collectives, local(): lax.all_to_all(first_step, 'chan', split_axis=1, concat_axis=3, tiled=True)  43.8 us
    gather x16, local copies, waits for them, and re-layouts, couple_terms(): source = jnp.take(field, couple[:, order], axis=1)  41 us
    select_n x12, other arithmetic, couple_terms(): source = jnp.take(field, couple[:, order], axis=1)  38.4 us
    dot_general x2, matrix products, radial_product(): jnp.einsum('ak,pckb->pcab', radial_op, block, precision=lax.Precision.HIG...  31.2 us
    unnamed x155, local copies, waits for them, and re-layouts  20.7 us
    all_to_all x2, waiting for transfers between devices, local(): lax.all_to_all(mirrored, 'chan', split_axis=3, concat_axis=1, tiled=True)  17.8 us
  transfers between devices with their start and end apart: 7, of which 6 were waited for; matrix products, arithmetic and copies ran while one was open for 30% of the time, Pallas kernels for 0%

commit v1 on v0

v1 whole, which is shorter than its diff:
```python
import functools

import jax
import jax.numpy as jnp
from jax import lax
from jax.experimental import pallas as pl
from jax.experimental.pallas import tpu as pltpu
from jax.sharding import PartitionSpec as P

NR = 1536
CH = 16
MULT = 8
DEV = 128
GRP = 8
STR = 16
COLS = 12
LANES = 128
ROWS = 384
WIRE = 4608
EACH = 36


def swap_groups(regs):
    lane = lax.broadcasted_iota(jnp.int32, (8, LANES), 1)
    regs = list(regs)
    for bit in (1, 2, 4, 8):
        upper = (lane & (8 * bit)) != 0
        for i in range(16):
            if i & bit:
                continue
            low, high = regs[i], regs[i | bit]
            regs[i] = jnp.where(upper, pltpu.roll(high, 8 * bit, 1), low)
            regs[i | bit] = jnp.where(upper, high, pltpu.roll(low, LANES - 8 * bit, 1))
    return regs


def row_of(part, y):
    return (y // 4) * 8 + part * 4 + y % 4


def params(mib=48):
    return pltpu.CompilerParams(vmem_limit_bytes=mib << 20)


def cost(flops, moved):
    return pl.CostEstimate(flops=flops, bytes_accessed=moved, transcendentals=0)


def pack_input_kernel(in_ref, out_ref):
    for j in range(3):
        regs = []
        for i in range(16):
            pc, ya = divmod(16 * j + i, COLS)
            regs.append(in_ref[pl.ds(pc * 96 + ya, 8, stride=COLS), :])
        out_ref[pl.ds(j, LANES, stride=3), :] = jnp.concatenate(regs, axis=0).T


def pack_input(wave):
    return pl.pallas_call(
        pack_input_kernel,
        out_shape=jax.ShapeDtypeStruct((WIRE, LANES), jnp.float32),
        grid=(COLS,),
        in_specs=[pl.BlockSpec((ROWS, LANES), lambda i: (0, i))],
        out_specs=pl.BlockSpec((ROWS, LANES), lambda i: (i, 0)),
        compiler_params=params(),
        name="pack_input",
    )(wave)


def order_operator_kernel(in_ref, high_ref, low_ref, held):
    step = pl.program_id(0)

    @pl.when(step < COLS)
    def _():
        for y in range(COLS):
            block = in_ref[pl.ds(y, LANES, stride=COLS), :].T
            held[y, pl.ds(pl.multiple_of(step * LANES, LANES), LANES), :] = block

    @pl.when(step >= COLS)
    def _():
        y = step - COLS
        for ya in range(COLS):
            block = held[y, pl.ds(ya, LANES, stride=COLS), :]
            high = block.astype(jnp.bfloat16)
            high_ref[ya * LANES : (ya + 1) * LANES, :] = high
            low_ref[ya * LANES : (ya + 1) * LANES, :] = (
                block - high.astype(jnp.float32)
            ).astype(jnp.bfloat16)


def order_operator(radial_op):
    out = jax.ShapeDtypeStruct((NR, NR), jnp.bfloat16)
    spec = pl.BlockSpec((NR, LANES), lambda i: (0, jnp.maximum(i - COLS, 0)))
    return pl.pallas_call(
        order_operator_kernel,
        out_shape=(out, out),
        grid=(2 * COLS,),
        in_specs=[pl.BlockSpec((NR, LANES), lambda i: (0, jnp.minimum(i, COLS - 1)))],
        out_specs=(spec, spec),
        scratch_shapes=[pltpu.VMEM((COLS, NR, LANES), jnp.float32)],
        compiler_params=params(),
        cost_estimate=cost(1 << 24, 4 * NR * NR * 2),
        name="order_operator",
    )(radial_op)


def split_terms(tiles_ref, high, low):
    for tile in range(COLS):
        block = tiles_ref[tile]
        upper = block.astype(jnp.bfloat16)
        high[:, tile * LANES : (tile + 1) * LANES] = upper
        low[:, tile * LANES : (tile + 1) * LANES] = (
            block - upper.astype(jnp.float32)
        ).astype(jnp.bfloat16)


def radial_step(step, high, low, op_high_ref, op_low_ref, image_ref, wire_ref):
    op_high = op_high_ref[...]
    image = jnp.dot(high[...], op_high, preferred_element_type=jnp.float32)
    image += jnp.dot(low[...], op_high, preferred_element_type=jnp.float32)
    image += jnp.dot(high[...], op_low_ref[...], preferred_element_type=jnp.float32)
    for half in range(2):
        block = image[:, half * LANES : (half + 1) * LANES]
        image_ref[half] = block
        for j in range(3):
            regs = [block[24 * c + 8 * j : 24 * c + 8 * j + 8, :] for c in range(CH)]
            start = (step * 2 + half) * 3 + j
            wire_ref[pl.ds(start, LANES, stride=EACH), :] = jnp.concatenate(regs, axis=0).T


def first_image_kernel(
    recv_ref, op_high_ref, op_low_ref, field_ref, image_ref, wire_ref, high, low
):
    step = pl.program_id(0)

    @pl.when(step == 0)
    def _():
        for y in range(COLS):
            for j in range(3):
                regs = swap_groups(
                    recv_ref[pl.ds(s * EACH + y * 3 + j, 8, stride=STR * EACH), :]
                    for s in range(STR)
                )
                for i in range(16):
                    pc, ya = divmod(16 * j + i, COLS)
                    start = (pc % 2) * 24 + row_of(pc // 2, y)
                    field_ref[ya, pl.ds(start, 8, stride=48), :] = regs[i]
        split_terms(field_ref, high, low)

    radial_step(step, high, low, op_high_ref, op_low_ref, image_ref, wire_ref)


TILES = jax.ShapeDtypeStruct((COLS, ROWS, LANES), jnp.float32)
SENT = jax.ShapeDtypeStruct((WIRE, LANES), jnp.float32)
SMEM = pl.BlockSpec(memory_space=pltpu.SMEM)


def whole(shape):
    return pl.BlockSpec(shape, lambda i: (0,) * len(shape))


OP_SPEC = pl.BlockSpec((NR, 2 * LANES), lambda i: (0, i))
PAIR_SPEC = pl.BlockSpec((2, ROWS, LANES), lambda i: (i, 0, 0))
FLOPS = 2 * 3 * ROWS * NR * NR


def first_image(recv, op_high, op_low):
    return pl.pallas_call(
        first_image_kernel,
        out_shape=(TILES, TILES, SENT),
        grid=(COLS // 2,),
        in_specs=[whole((WIRE, LANES)), OP_SPEC, OP_SPEC],
        out_specs=(whole(TILES.shape), PAIR_SPEC, whole(SENT.shape)),
        scratch_shapes=[
            pltpu.VMEM((ROWS, NR), jnp.bfloat16),
            pltpu.VMEM((ROWS, NR), jnp.bfloat16),
        ],
        compiler_params=params(),
        cost_estimate=cost(FLOPS, 20 << 20),
        name="first_image",
    )(recv, op_high, op_low)


def position_of(step, device):
    lane = lax.broadcasted_iota(jnp.int32, (24, LANES), 1)
    row = lax.broadcasted_iota(jnp.int32, (24, LANES), 0)
    return 12 * lane + step, 12 * device + (row // 8) * 4 + row % 4


def couple_kernel(device_ref, coupling_ref, couple_ref, field_ref, image_ref, out_ref, turned):
    step = pl.program_id(0)
    a, b = position_of(step, device_ref[0])
    first = a.astype(jnp.float32) * (8.0 / NR)
    second = b.astype(jnp.float32) * (8.0 / NR)
    greater = jnp.maximum(first, second)
    inverse = 1.0 / jnp.sqrt(greater * greater + 1.0)
    ratio = jnp.minimum(first, second) * inverse
    row = lax.broadcasted_iota(jnp.int32, (8, LANES), 0)
    sign = jnp.where(row < 4, -1.0, 1.0)
    for c in range(CH):
        for t in range(3):
            block = field_ref[0, c, 8 * t : 8 * t + 8, :]
            turned[c, 8 * t : 8 * t + 8, :] = pltpu.roll(block, 4, 0) * sign

    @pl.loop(0, CH)
    def _(c):
        total = jnp.zeros((24, LANES), jnp.float32)
        for order in reversed(range(MULT)):
            source = couple_ref[c, order]
            term = coupling_ref[0, c, order] * field_ref[0, source]
            term += coupling_ref[1, c, order] * turned[source]
            total = total * ratio + term
        out_ref[0, c] = image_ref[0, c] + total * inverse


def couple_terms(device, coupling, couple, field, image):
    shape = (COLS, CH, 24, LANES)
    spec = pl.BlockSpec((1,) + shape[1:], lambda i: (i, 0, 0, 0))
    out = pl.pallas_call(
        couple_kernel,
        out_shape=jax.ShapeDtypeStruct(shape, jnp.float32),
        grid=(COLS,),
        in_specs=[SMEM, SMEM, SMEM, spec, spec],
        out_specs=spec,
        scratch_shapes=[pltpu.VMEM((CH, 24, LANES), jnp.float32)],
        compiler_params=params(),
        cost_estimate=cost(1 << 28, 8 << 20),
        name="couple_terms",
    )(device, coupling, couple, field.reshape(shape), image.reshape(shape))
    return out.reshape(TILES.shape)


def unpack_mirror(recv_ref, mirror, block):
    for y in range(COLS):
        for j in range(3):
            block[...] = recv_ref[pl.ds(y * 3 + j, LANES, stride=EACH), :].T
            for part in range(2):
                for k in range(4):
                    mirror[4 * j + k, pl.ds(row_of(part, y), CH, stride=24), :] = block[
                        pl.ds(part * 4 + k, CH, stride=8), :
                    ]


def live_sum(tile, c, device_ref, partner_ref, extent_ref, direct_ref, mirror):
    a, b = position_of(tile, device_ref[0])
    extent = extent_ref[c]
    here = pl.ds(pl.multiple_of(c * 24, 8), 24)
    there = pl.ds(pl.multiple_of(partner_ref[c] * 24, 8), 24)
    total = direct_ref[tile, here, :] + mirror[tile, there, :]
    return here, jnp.where((a < extent) & (b < extent), total, 0.0)


def pack_output(tiles_ref, wire_ref):
    for tile in range(COLS):
        for t in range(3):
            regs = swap_groups(
                tiles_ref[tile, 24 * c + 8 * t : 24 * c + 8 * t + 8, :] for c in range(CH)
            )
            for s in range(STR):
                start = s * 288 + tile * 24 + t * 8
                wire_ref[start : start + 8, :] = regs[s]


def second_image_kernel(
    device_ref,
    partner_ref,
    extent_ref,
    recv_ref,
    direct_ref,
    op_high_ref,
    op_low_ref,
    field_ref,
    image_ref,
    wire_ref,
    output_ref,
    high,
    low,
    mirror,
    block,
):
    step = pl.program_id(0)

    @pl.when(step == 0)
    def _():
        unpack_mirror(recv_ref, mirror, block)

        @pl.loop(0, COLS)
        def _(tile):
            @pl.loop(0, CH)
            def _(c):
                here, total = live_sum(
                    tile, c, device_ref, partner_ref, extent_ref, direct_ref, mirror
                )
                field_ref[tile, here, :] = total

        split_terms(field_ref, high, low)
        pack_output(field_ref, output_ref)

    radial_step(step, high, low, op_high_ref, op_low_ref, image_ref, wire_ref)


def second_image(device, partner, extent, recv, direct, op_high, op_low):
    return pl.pallas_call(
        second_image_kernel,
        out_shape=(TILES, TILES, SENT, SENT),
        grid=(COLS // 2,),
        in_specs=[
            SMEM,
            SMEM,
            SMEM,
            whole(SENT.shape),
            whole(TILES.shape),
            OP_SPEC,
            OP_SPEC,
        ],
        out_specs=(whole(TILES.shape), PAIR_SPEC, whole(SENT.shape), whole(SENT.shape)),
        scratch_shapes=[
            pltpu.VMEM((ROWS, NR), jnp.bfloat16),
            pltpu.VMEM((ROWS, NR), jnp.bfloat16),
            pltpu.VMEM(TILES.shape, jnp.float32),
            pltpu.VMEM((LANES, LANES), jnp.float32),
        ],
        compiler_params=params(),
        cost_estimate=cost(FLOPS, 25 << 20),
        name="second_image",
    )(device, partner, extent, recv, direct, op_high, op_low)


def second_vector_kernel(
    device_ref,
    partner_ref,
    extent_ref,
    recv_ref,
    direct_ref,
    field_ref,
    output_ref,
    mirror,
    result,
    block,
):
    unpack_mirror(recv_ref, mirror, block)

    @pl.loop(0, COLS)
    def _(tile):
        @pl.loop(0, CH)
        def _(c):
            here, total = live_sum(
                tile, c, device_ref, partner_ref, extent_ref, direct_ref, mirror
            )
            result[tile, here, :] = 2.0 * total - field_ref[tile, here, :]

    pack_output(result, output_ref)


def second_vector(device, partner, extent, recv, direct, field):
    return pl.pallas_call(
        second_vector_kernel,
        out_shape=SENT,
        grid=(1,),
        in_specs=[
            SMEM,
            SMEM,
            SMEM,
            whole(SENT.shape),
            whole(TILES.shape),
            whole(TILES.shape),
        ],
        out_specs=whole(SENT.shape),
        scratch_shapes=[
            pltpu.VMEM(TILES.shape, jnp.float32),
            pltpu.VMEM(TILES.shape, jnp.float32),
            pltpu.VMEM((LANES, LANES), jnp.float32),
        ],
        compiler_params=params(),
        cost_estimate=cost(1 << 24, 10 << 20),
        name="second_vector",
    )(device, partner, extent, recv, direct, field)


def place_output_kernel(recv_ref, out_ref, rows, left, right):
    part = pl.program_id(0)
    for ya in range(COLS):
        for s in range(STR):
            for t in range(3):
                start = s * 288 + ya * 24 + t * 8
                block = recv_ref[start : start + 8, :]
                block = jnp.where(part == 0, block[:4], block[4:])
                rows[12 * s + 4 * t : 12 * s + 4 * t + 4, :] = block
        turned = rows[...].T
        left[pl.ds(ya, LANES, stride=COLS), :] = turned[:, :LANES]
        right[pl.ds(ya, LANES, stride=COLS), :] = turned[:, LANES:]
    out_ref[0, :, :LANES] = left[...]
    out_ref[0, :, LANES:] = right[:, :64]


def place_output(recv):
    out = pl.pallas_call(
        place_output_kernel,
        out_shape=jax.ShapeDtypeStruct((2, NR, 192), jnp.float32),
        grid=(2,),
        in_specs=[whole(SENT.shape)],
        out_specs=pl.BlockSpec((1, NR, 192), lambda i: (i, 0, 0)),
        scratch_shapes=[
            pltpu.VMEM((256, LANES), jnp.float32),
            pltpu.VMEM((NR, LANES), jnp.float32),
            pltpu.VMEM((NR, LANES), jnp.float32),
        ],
        compiler_params=params(),
        cost_estimate=cost(1 << 24, 5 << 20),
        name="place_output",
    )(recv)
    return out.reshape(2, CH, 96, 192)


def exchange_all(sent):
    sent = sent.reshape(DEV, 9, 4, LANES)
    recv = lax.all_to_all(sent, ("chan", "strip"), 0, 0, tiled=True)
    return recv.reshape(WIRE, LANES)


def exchange_strip(sent):
    sent = sent.reshape(STR, WIRE // STR, LANES)
    return lax.all_to_all(sent, "strip", 0, 0, tiled=True).reshape(WIRE, LANES)


def local(wave_field, radial_op, coupling, couple, partner, extent):
    device = (lax.axis_index("chan") * STR + lax.axis_index("strip")).reshape(1)
    op_high, op_low = order_operator(radial_op)
    recv = exchange_all(pack_input(wave_field.reshape(ROWS, NR)))
    field, image, sent = first_image(recv, op_high, op_low)
    recv = exchange_all(sent)
    direct = couple_terms(device, coupling, couple, field, image)
    first, image, sent, output = second_image(
        device, partner, extent, recv, direct, op_high, op_low
    )
    recv = exchange_all(sent)
    direct = couple_terms(device, coupling, couple, first, image)
    first_step = place_output(exchange_strip(output))
    output = second_vector(device, partner, extent, recv, direct, field)
    second_step = place_output(exchange_strip(output))
    return (first_step, second_step)


def solution(mesh):
    placed = (P(None, "chan", "strip", None), P(), P(), P(), P(), P())
    return jax.shard_map(
        local,
        mesh=mesh,
        in_specs=placed,
        out_specs=(P(None, None, "strip", "chan"), P(None, None, "strip", "chan")),
        check_vma=False,
    )
```

time: 550 us -> 250 us (0.45); the launches traced: 539 us -> 248 us
  local copies, waits for them, and re-layouts: 155 us -> 11.3 us
  Pallas kernels: 0 us -> 105 us
  blocking collectives: 134 us -> 38.3 us
  other arithmetic: 79.5 us -> 0 us
  waiting for transfers between devices: 101 us -> 66.3 us
  matrix products: 31.2 us -> 0 us
  starting transfers between devices: 36.9 us -> 27 us
    pallas_call x0 -> x9, Pallas kernels: none -> 105 us  [the longest x1 24.4 us: second_image(): pl.pallas_call(second_image_kernel, out_shape=(TILES, TILES, SENT, SENT),...]
    all_to_all x3 -> x1, blocking collectives: 134 us -> 38.3 us  [exchange_all(): recv = lax.all_to_all(sent, ('chan', 'strip'), 0, 0, tiled=True)]
    all_to_all x14 -> x0, local copies, waits for them, and re-layouts: 66 us -> none  [the longest x4 16.5 us: both_terms(): lax.all_to_all(image, 'strip', split_axis=2, concat_axis=3, tiled=True)]
    gather x18 -> x0, local copies, waits for them, and re-layouts: 49.9 us -> none  [the longest x16 41 us: couple_terms(): source = jnp.take(field, couple[:, order], axis=1)]
    select_n x14 -> x0, other arithmetic: 38.8 us -> none  [the longest x12 38.4 us: couple_terms(): source = jnp.take(field, couple[:, order], axis=1)]
    all_to_all x7 -> x4, waiting for transfers between devices: 101 us -> 66.3 us  [the longest x2 37.9 us: exchange_all(): recv = lax.all_to_all(sent, ('chan', 'strip'), 0, 0, tiled=True)]
    add x8 -> x0, other arithmetic: 31.8 us -> none  [the longest x2 14.6 us: couple_terms(): imag_part + pots[order] * (c_real * source[1] + c_imag * source[0])]
    dot_general x2 -> x0, matrix products: 31.2 us -> none  [radial_product(): jnp.einsum('ak,pckb->pcab', radial_op, block, precision=lax.Precision.HIG...]
  transfers between devices with their start and end apart: 7 -> 4, of which waited for: 6 -> 4; matrix products, arithmetic and copies ran while one was open for 30% -> 0% of each run, Pallas kernels for 0% -> 21%
where the time goes in v1:
time: 250 us; the launch traced here: 248 us
  Pallas kernels  105 us (42%)
  waiting for transfers between devices  66.3 us (27%)
  blocking collectives  38.3 us (15%)
  starting transfers between devices  27 us (11%)
  local copies, waits for them, and re-layouts  11.3 us (5%)
    all_to_all x1, blocking collectives, exchange_all(): recv = lax.all_to_all(sent, ('chan', 'strip'), 0, 0, tiled=True)  38.3 us
    all_to_all x2, waiting for transfers between devices, exchange_all(): recv = lax.all_to_all(sent, ('chan', 'strip'), 0, 0, tiled=True)  37.9 us
    all_to_all x2, waiting for transfers between devices, exchange_strip(): return lax.all_to_all(sent, 'strip', 0, 0, tiled=True).reshape(WIRE, LANES)  28.4 us
    pallas_call x1, Pallas kernels, second_image(): pl.pallas_call(second_image_kernel, out_shape=(TILES, TILES, SENT, SENT),...  24.4 us
    pallas_call x1, Pallas kernels, first_image(): pl.pallas_call(first_image_kernel, out_shape=(TILES, TILES, SENT), grid=(...  19.8 us
    pallas_call x2, Pallas kernels, couple_terms(): pl.pallas_call(couple_kernel, out_shape=jax.ShapeDtypeStruct(shape, jnp.f...  18.7 us
    all_to_all x2, starting transfers between devices, exchange_all(): recv = lax.all_to_all(sent, ('chan', 'strip'), 0, 0, tiled=True)  17.3 us
    pallas_call x1, Pallas kernels, second_vector(): pl.pallas_call(second_vector_kernel, out_shape=SENT, grid=(1,), in_specs=...  15.3 us
  transfers between devices with their start and end apart: 4, of which 4 were waited for; matrix products, arithmetic and copies ran while one was open for 0% of the time, Pallas kernels for 21%

profile of v1, /device:TPU:1, one launch (start us, length us, event | category | flops | bytes accessed | tf_op | source)
XLA Modules:
  0.0 248.2 jit_solution(17961568648882059646)
XLA Ops:
  0.6 0.0 copy-start.2
  0.6 1.7 copy-done.2
  2.3 5.2 %pack_input.1 = f32[4608,128]{1,0:T(8,128)} custom-call(f32[384,1536]{1,0:T(8,128)S(1)} %bitcast.24), custom_call_target="tpu_custom_call" | custom-call | tf_op jit(solution)/shard_map/pack_input/pallas_call | solution.py:59
  7.5 11.5 %all-to-all-start = ((f32[128,9,4,128]{3,2,1,0:T(4,128)}), f32[128,9,4,128]{3,2,1,0:T(4,128)S(1)}, u32[]{:S(2)}, u32[]{:S(2)}) async-start(f32[128,9,4,128]{3,2,1,0:T(4,128)} %bitcast.2), calls=%async_computation | async-start | bytes 4718592 | tf_op jit(solution)/shard_map/all_to_all | solution.py:417
  19.0 15.0 %order_operator.1 = (bf16[1536,1536]{1,0:T(8,128)(2,1)S(1)}, bf16[1536,1536]{1,0:T(8,128)(2,1)}) custom-call(f32[1536,1536]{1,0:T(8,128)} %in_ref.1), custom_call_target="tpu_custom_call" | custom-call | flops 16777216 | bytes 18874368 | tf_op jit(solution)/shard_map/order_operator/pallas_call | solution.py:94
  34.0 2.2 copy-done.10
  36.2 15.9 %all-to-all-done = f32[128,9,4,128]{3,2,1,0:T(4,128)S(1)} async-done(((f32[128,9,4,128]{3,2,1,0:T(4,128)}), f32[128,9,4,128]{3,2,1,0:T(4,128)S(1)}, u32[]{:S(2)}, u32[]{:S(2)}) %all-to-all-start) | async-done | bytes 2359328 | tf_op jit(solution)/shard_map/all_to_all | solution.py:417
  52.1 1.4 copy-done.11
  53.5 19.8 %first_image.1 = (f32[12,384,128]{2,1,0:T(8,128)S(1)}, f32[12,384,128]{2,1,0:T(8,128)S(1)}, f32[4608,128]{1,0:T(8,128)}) custom-call(f32[4608,128]{1,0:T(8,128)} %bitcast.33, bf16[1536,1536]{1,0:T(8,128)(2,1)} %copy-done.10, bf16[1536,1536]{1,0:T(8,128)(2,1)} %get-tuple-element.12.op_low_ref), custom_call_target="tpu_custom_call" | custom-call | flops 5435817984 | bytes 20971520 | tf_op jit(solution)/shard_map/first_image/pallas_call | solution.py:168
  73.3 1.4 copy-done.3
  74.7 5.8 %all-to-all-start.1 = ((f32[128,9,4,128]{3,2,1,0:T(4,128)}), f32[128,9,4,128]{3,2,1,0:T(4,128)}, u32[]{:S(2)}, u32[]{:S(2)}) async-start(f32[128,9,4,128]{3,2,1,0:T(4,128)} %bitcast.31), calls=%async_computation.1 | async-start | bytes 4718592 | tf_op jit(solution)/shard_map/all_to_all | solution.py:417
  80.5 0.0 copy-done.13
  80.5 0.1 copy.9.couple_ref
  80.5 0.0 copy-done.12
  80.5 0.1 copy.8.coupling_ref
  80.6 9.4 %couple_terms.2 = f32[12,16,24,128]{3,2,1,0:T(8,128)S(1)} custom-call(s32[1]{0:T(128)} %bitcast.device_ref, f32[2,16,8]{2,1,0:T(8,128)S(1)} %copy.8.coupling_ref, s32[16,8]{1,0:T(8,128)S(1)} %copy.9.couple_ref, f32[12,16,24,128]{3,2,1,0:T(8,128)S(1)} %bitcast.21, f32[12,16,24,128]{3,2,1,0:T(8,128)} %bitcast.25), custom_call_target="tpu_custom_call" | custom-call | flops 268435456 | bytes 8388608 | tf_op jit(solution)/shard_map/couple_terms/pallas_call | solution.py:219
  90.0 0.0 copy-start.7
  90.0 1.4 copy-done.7
  91.4 22.0 %all-to-all-done.1 = f32[128,9,4,128]{3,2,1,0:T(4,128)} async-done(((f32[128,9,4,128]{3,2,1,0:T(4,128)}), f32[128,9,4,128]{3,2,1,0:T(4,128)}, u32[]{:S(2)}, u32[]{:S(2)}) %all-to-all-start.1) | async-done | bytes 2359328 | tf_op jit(solution)/shard_map/all_to_all | solution.py:417
  113.4 24.4 %second_image.1 = (f32[12,384,128]{2,1,0:T(8,128)S(1)}, f32[12,384,128]{2,1,0:T(8,128)S(1)}, f32[4608,128]{1,0:T(8,128)}, f32[4608,128]{1,0:T(8,128)}) custom-call(s32[1]{0:T(128)} %bitcast.device_ref, s32[16]{0:T(128)S(1)} %copy-done.8, s32[16]{0:T(128)S(1)} %copy-done.9, f32[4608,128]{1,0:T(8,128)} %bitcast.5.recv_ref, f32[12,384,128]{2,1,0:T(8,128)} %bitcast.28, ...), custom_call_target="tpu_custom_call" | custom-call | flops 5435817984 | bytes 26214400 | tf_op jit(solution)/shard_map/second_image/pallas_call | solution.py:303
  137.8 38.3 %all_to_all.25 = f32[128,9,4,128]{3,2,1,0:T(4,128)S(1)} all-to-all(f32[128,9,4,128]{3,2,1,0:T(4,128)} %bitcast.34), channel_id=1, replica_groups=mesh['chan'=8,'strip'=16] {'chan','strip'}, dimensions={0} | all-to-all | bytes 4718592 | tf_op jit(solution)/shard_map/all_to_all | solution.py:417
  176.1 5.3 %all-to-all-start.2 = ((f32[16,288,128]{2,1,0:T(8,128)}), f32[16,288,128]{2,1,0:T(8,128)}, u32[]{:S(2)}, u32[]{:S(2)}) async-start(f32[16,288,128]{2,1,0:T(8,128)} %bitcast.32), calls=%async_computation.2 | async-start | bytes 4718592 | tf_op jit(solution)/shard_map/all_to_all | solution.py:423
  181.4 1.7 copy-done.5
  183.1 9.3 %couple_terms.3 = f32[12,16,24,128]{3,2,1,0:T(8,128)S(1)} custom-call(s32[1]{0:T(128)} %bitcast.device_ref, f32[2,16,8]{2,1,0:T(8,128)S(1)} %copy.8.coupling_ref, s32[16,8]{1,0:T(8,128)S(1)} %copy.9.couple_ref, f32[12,16,24,128]{3,2,1,0:T(8,128)S(1)} %bitcast.26, f32[12,16,24,128]{3,2,1,0:T(8,128)} %bitcast.27), custom_call_target="tpu_custom_call" | custom-call | flops 268435456 | bytes 8388608 | tf_op jit(solution)/shard_map/couple_terms/pallas_call | solution.py:219
  192.4 0.0 copy-start.1
  192.4 1.4 copy-done.1
  193.8 15.3 %second_vector.1 = f32[4608,128]{1,0:T(8,128)} custom-call(s32[1]{0:T(128)} %bitcast.device_ref, s32[16]{0:T(128)S(1)} %copy-done.8, s32[16]{0:T(128)S(1)} %copy-done.9, f32[4608,128]{1,0:T(8,128)S(1)} %bitcast.20, f32[12,384,128]{2,1,0:T(8,128)} %bitcast.22, f32[12,384,128]{2,1,0:T(8,128)} %copy-done), custom_call_target="tpu_custom_call" | custom-call | flops 16777216 | bytes 10485760 | tf_op jit(solution)/shard_map/second_vector/pallas_call | solution.py:356
  209.1 2.4 all-to-all-done.2
  211.5 4.4 %all-to-all-start.4 = ((f32[16,288,128]{2,1,0:T(8,128)}), f32[16,288,128]{2,1,0:T(8,128)S(1)}, u32[]{:S(2)}, u32[]{:S(2)}) async-start(f32[16,288,128]{2,1,0:T(8,128)} %bitcast.17), calls=%async_computation.4 | async-start | bytes 4718592 | tf_op jit(solution)/shard_map/all_to_all | solution.py:423
  215.9 4.0 %place_output.2 = f32[2,1536,192]{2,1,0:T(8,128)} custom-call(f32[4608,128]{1,0:T(8,128)} %bitcast.10.recv_ref), custom_call_target="tpu_custom_call" | custom-call | flops 16777216 | bytes 5242880 | tf_op jit(solution)/shard_map/place_output/pallas_call | solution.py:397
  219.9 26.0 %all-to-all-done.4 = f32[16,288,128]{2,1,0:T(8,128)S(1)} async-done(((f32[16,288,128]{2,1,0:T(8,128)}), f32[16,288,128]{2,1,0:T(8,128)S(1)}, u32[]{:S(2)}, u32[]{:S(2)}) %all-to-all-start.4) | async-done | bytes 2359328 | tf_op jit(solution)/shard_map/all_to_all | solution.py:423
  245.9 2.3 place_output.3
  (16 shorter events, 0.0 us)
Async XLA Ops:
  0.6 1.7 copy-start.2
  7.5 44.6 %all-to-all-start = ((f32[128,9,4,128]{3,2,1,0:T(4,128)}), f32[128,9,4,128]{3,2,1,0:T(4,128)S(1)}, u32[]{:S(2)}, u32[]{:S(2)}) async-start(f32[128,9,4,128]{3,2,1,0:T(4,128)} %bitcast.2), calls=%async_computation | async-start | bytes 4718592 | tf_op jit(solution)/shard_map/all_to_all | solution.py:417
  34.0 2.2 copy-start.10
  52.1 1.4 copy-start.11
  73.3 1.4 copy-start.3
  74.7 6.0 %copy-start = (f32[12,384,128]{2,1,0:T(8,128)}, f32[12,384,128]{2,1,0:T(8,128)S(1)}, u32[]{:S(2)}) copy-start(f32[12,384,128]{2,1,0:T(8,128)S(1)} %get-tuple-element.14.field_ref) | copy-start | bytes 7077892
  74.7 5.8 %copy-start.13 = (s32[16,8]{0,1:T(8,128)S(1)}, s32[16,8]{0,1:T(8,128)}, u32[]{:S(2)}) copy-start(s32[16,8]{0,1:T(8,128)} %param.9) | copy-start | bytes 1540
  74.7 5.9 %copy-start.12 = (f32[2,16,8]{1,2,0:T(8,128)S(1)}, f32[2,16,8]{1,2,0:T(8,128)}, u32[]{:S(2)}) copy-start(f32[2,16,8]{1,2,0:T(8,128)} %param.8) | copy-start | bytes 3076
  74.7 38.7 %all-to-all-start.1 = ((f32[128,9,4,128]{3,2,1,0:T(4,128)}), f32[128,9,4,128]{3,2,1,0:T(4,128)}, u32[]{:S(2)}, u32[]{:S(2)}) async-start(f32[128,9,4,128]{3,2,1,0:T(4,128)} %bitcast.31), calls=%async_computation.1 | async-start | bytes 4718592 | tf_op jit(solution)/shard_map/all_to_all | solution.py:417
  80.6 32.8 %copy-start.8 = (s32[16]{0:T(128)S(1)}, s32[16]{0:T(128)}, u32[]{:S(2)}) copy-start(s32[16]{0:T(128)} %partner_ref.3) | copy-start | bytes 196
  80.6 32.8 %copy-start.9 = (s32[16]{0:T(128)S(1)}, s32[16]{0:T(128)}, u32[]{:S(2)}) copy-start(s32[16]{0:T(128)} %extent_ref.3) | copy-start | bytes 196
  90.0 1.4 copy-start.7
  137.8 38.3 %copy-start.4 = (f32[12,384,128]{2,1,0:T(8,128)}, f32[12,384,128]{2,1,0:T(8,128)S(1)}, u32[]{:S(2)}) copy-start(f32[12,384,128]{2,1,0:T(8,128)S(1)} %get-tuple-element.18) | copy-start | bytes 7077892
  137.8 38.3 %copy-start.6 = (f32[12,384,128]{2,1,0:T(8,128)}, f32[12,384,128]{2,1,0:T(8,128)S(1)}, u32[]{:S(2)}) copy-start(f32[12,384,128]{2,1,0:T(8,128)S(1)} %get-tuple-element.19) | copy-start | bytes 7077892
  176.1 35.4 %all-to-all-start.2 = ((f32[16,288,128]{2,1,0:T(8,128)}), f32[16,288,128]{2,1,0:T(8,128)}, u32[]{:S(2)}, u32[]{:S(2)}) async-start(f32[16,288,128]{2,1,0:T(8,128)} %bitcast.32), calls=%async_computation.2 | async-start | bytes 4718592 | tf_op jit(solution)/shard_map/all_to_all | solution.py:423
  181.4 1.7 copy-start.5
  192.4 1.4 copy-start.1
  211.5 34.4 %all-to-all-start.4 = ((f32[16,288,128]{2,1,0:T(8,128)}), f32[16,288,128]{2,1,0:T(8,128)S(1)}, u32[]{:S(2)}, u32[]{:S(2)}) async-start(f32[16,288,128]{2,1,0:T(8,128)} %bitcast.17), calls=%async_computation.4 | async-start | bytes 4718592 | tf_op jit(solution)/shard_map/all_to_all | solution.py:423

commit v2 on v1

v2 whole, which is shorter than its diff:
```python
import functools

import jax
import jax.numpy as jnp
from jax import lax
from jax.experimental import pallas as pl
from jax.experimental.pallas import tpu as pltpu
from jax.sharding import PartitionSpec as P

NR = 1536
CH = 16
MULT = 8
DEV = 128
GRP = 8
STR = 16
COLS = 12
LANES = 128
ROWS = 384
WIRE = 4608
EACH = 36


TILES = pltpu.HBM((COLS, ROWS, LANES), jnp.float32)
SENT = pltpu.HBM((WIRE, LANES), jnp.float32)
SMEM = pl.BlockSpec(memory_space=pltpu.SMEM)
HBM = pl.BlockSpec(memory_space=pltpu.HBM)
VMEM = pl.BlockSpec(memory_space=pltpu.VMEM)
SENT_SPEC = pl.BlockSpec((WIRE, LANES), lambda i: (0, 0))
TILES_SPEC = pl.BlockSpec((COLS, ROWS, LANES), lambda i: (0, 0, 0))
HELD = pltpu.VMEM((COLS, ROWS, LANES), jnp.float32)
TURN = 4
OP_SPEC = pl.BlockSpec((TURN, NR, LANES), lambda i: (i, 0, 0))
IMAGE_SPEC = pl.BlockSpec((TURN, ROWS, LANES), lambda i: (i, 0, 0))
FLOPS = 2 * 3 * ROWS * NR * NR


def swap_groups(regs):
    lane = lax.broadcasted_iota(jnp.int32, (8, LANES), 1)
    regs = list(regs)
    for bit in (1, 2, 4, 8):
        upper = (lane & (8 * bit)) != 0
        for i in range(16):
            if i & bit:
                continue
            low, high = regs[i], regs[i | bit]
            regs[i] = jnp.where(upper, pltpu.roll(high, 8 * bit, 1), low)
            regs[i | bit] = jnp.where(upper, high, pltpu.roll(low, LANES - 8 * bit, 1))
    return regs


def row_of(part, y):
    return (y // 4) * 8 + part * 4 + y % 4


def params(mib=20):
    return pltpu.CompilerParams(vmem_limit_bytes=mib << 20)


def hbm(*arrays):
    return [pltpu.with_memory_space_constraint(x, pltpu.HBM) for x in arrays]


def cost(flops, moved):
    return pl.CostEstimate(flops=flops, bytes_accessed=moved, transcendentals=0)


def pack_input_kernel(in_ref, out_ref):
    for tile in range(COLS):
        lanes = slice(tile * LANES, (tile + 1) * LANES)
        for j in range(3):
            block = in_ref[j * LANES : (j + 1) * LANES, lanes]
            out_ref[pl.ds(tile * ROWS + j, LANES, stride=3), :] = block.T


def pack_input(wave):
    return pl.pallas_call(
        pack_input_kernel,
        out_shape=SENT,
        grid=(1,),
        in_specs=[pl.BlockSpec((ROWS, NR), lambda i: (0, 0))],
        out_specs=SENT_SPEC,
        compiler_params=params(12),
        name="pack_input",
    )(*hbm(wave))


def order_operator_kernel(in_ref, high_ref, low_ref, held):
    step = pl.program_id(0)

    @pl.when(step < COLS)
    def _():
        for y in range(COLS):
            block = in_ref[pl.ds(y, LANES, stride=COLS), :].T
            held[y, pl.ds(pl.multiple_of(step * LANES, LANES), LANES), :] = block

    @pl.when(step >= COLS)
    def _():
        y = step - COLS
        for ya in range(COLS):
            block = held[y, pl.ds(ya, LANES, stride=COLS), :]
            high = block.astype(jnp.bfloat16)
            rows = slice(ya * LANES, (ya + 1) * LANES)
            high_ref[0, rows, :] = high
            low_ref[0, rows, :] = (block - high.astype(jnp.float32)).astype(jnp.bfloat16)


def order_operator(radial_op):
    out = pltpu.HBM((COLS, NR, LANES), jnp.bfloat16)
    spec = pl.BlockSpec((1, NR, LANES), lambda i: (jnp.maximum(i - COLS, 0), 0, 0))
    return pl.pallas_call(
        order_operator_kernel,
        out_shape=(out, out),
        grid=(2 * COLS,),
        in_specs=[pl.BlockSpec((NR, LANES), lambda i: (0, jnp.minimum(i, COLS - 1)))],
        out_specs=(spec, spec),
        scratch_shapes=[pltpu.VMEM((COLS, NR, LANES), jnp.float32)],
        compiler_params=params(),
        cost_estimate=cost(1 << 24, 4 * NR * NR * 2),
        name="order_operator",
    )(*hbm(radial_op))


def split_terms(tiles_ref, high, low):
    for tile in range(COLS):
        block = tiles_ref[tile]
        upper = block.astype(jnp.bfloat16)
        high[:, tile * LANES : (tile + 1) * LANES] = upper
        low[:, tile * LANES : (tile + 1) * LANES] = (
            block - upper.astype(jnp.float32)
        ).astype(jnp.bfloat16)


def radial_step(step, high, low, op_high_ref, op_low_ref, image_ref, wire_ref):
    op_high = jnp.concatenate([op_high_ref[i] for i in range(TURN)], axis=1)
    op_low = jnp.concatenate([op_low_ref[i] for i in range(TURN)], axis=1)
    image = jnp.dot(high[...], op_high, preferred_element_type=jnp.float32)
    image += jnp.dot(low[...], op_high, preferred_element_type=jnp.float32)
    image += jnp.dot(high[...], op_low, preferred_element_type=jnp.float32)
    for i in range(TURN):
        block = image[:, i * LANES : (i + 1) * LANES]
        image_ref[i] = block
        for j in range(3):
            regs = [block[24 * c + 8 * j : 24 * c + 8 * j + 8, :] for c in range(CH)]
            start = (step * TURN + i) * 3 + j
            wire_ref[pl.ds(start, LANES, stride=EACH), :] = jnp.concatenate(regs, axis=0).T


def unpack_input(recv_ref, field_ref, held):
    for s in range(STR):
        for j in range(3):
            rows = [
                recv_ref[pl.ds(s * EACH + y * 3 + j, 8, stride=STR * EACH), :]
                for y in range(COLS)
            ]
            start = s * ROWS + j * LANES
            held[start : start + LANES, :96] = jnp.concatenate(rows, axis=0).T
    for pc in range(4):
        for ya in range(COLS):
            rows = [
                held[pl.ds(s * ROWS + pc * 96 + ya, 8, stride=COLS), :] for s in range(STR)
            ]
            block = jnp.concatenate(rows, axis=0).T
            for y in range(COLS):
                start = (pc % 2) * 24 + row_of(pc // 2, y)
                field_ref[ya, pl.ds(start, 8, stride=48), :] = block[8 * y : 8 * y + 8, :]


def first_image_kernel(
    recv_ref,
    op_high_ref,
    op_low_ref,
    field_ref,
    image_ref,
    wire_ref,
    high,
    low,
    held,
    field,
    sem,
):
    step = pl.program_id(0)
    keep = pltpu.make_async_copy(field, field_ref, sem)

    @pl.when(step == 0)
    def _():
        unpack_input(recv_ref, field, held)
        keep.start()
        split_terms(field, high, low)

    radial_step(step, high, low, op_high_ref, op_low_ref, image_ref, wire_ref)

    @pl.when(step == COLS // TURN - 1)
    def _():
        keep.wait()


def first_image(recv, op_high, op_low):
    return pl.pallas_call(
        first_image_kernel,
        out_shape=(TILES, TILES, SENT),
        grid=(COLS // TURN,),
        in_specs=[VMEM, OP_SPEC, OP_SPEC],
        out_specs=(HBM, IMAGE_SPEC, SENT_SPEC),
        scratch_shapes=[
            pltpu.VMEM((ROWS, NR), jnp.bfloat16),
            pltpu.VMEM((ROWS, NR), jnp.bfloat16),
            pltpu.VMEM((STR * ROWS, LANES), jnp.float32),
            HELD,
            pltpu.SemaphoreType.DMA,
        ],
        compiler_params=params(32),
        cost_estimate=cost(FLOPS, 20 << 20),
        name="first_image",
    )(recv, *hbm(op_high, op_low))


def position_of(step, device):
    lane = lax.broadcasted_iota(jnp.int32, (24, LANES), 1)
    row = lax.broadcasted_iota(jnp.int32, (24, LANES), 0)
    return 12 * lane + step, 12 * device + (row // 8) * 4 + row % 4


def couple_kernel(device_ref, coupling_ref, couple_ref, field_ref, image_ref, out_ref, turned):
    step = pl.program_id(0)
    a, b = position_of(step, device_ref[0])
    first = a.astype(jnp.float32) * (8.0 / NR)
    second = b.astype(jnp.float32) * (8.0 / NR)
    greater = jnp.maximum(first, second)
    inverse = 1.0 / jnp.sqrt(greater * greater + 1.0)
    ratio = jnp.minimum(first, second) * inverse
    row = lax.broadcasted_iota(jnp.int32, (8, LANES), 0)
    sign = jnp.where(row < 4, -1.0, 1.0)
    for c in range(CH):
        for t in range(3):
            block = field_ref[0, c, 8 * t : 8 * t + 8, :]
            turned[c, 8 * t : 8 * t + 8, :] = pltpu.roll(block, 4, 0) * sign

    @pl.loop(0, CH)
    def _(c):
        total = jnp.zeros((24, LANES), jnp.float32)
        for order in reversed(range(MULT)):
            source = couple_ref[c, order]
            term = coupling_ref[0, c, order] * field_ref[0, source]
            term += coupling_ref[1, c, order] * turned[source]
            total = total * ratio + term
        out_ref[0, c] = image_ref[0, c] + total * inverse


def couple_terms(device, coupling, couple, field, image):
    shape = (COLS, CH, 24, LANES)
    spec = pl.BlockSpec((1,) + shape[1:], lambda i: (i, 0, 0, 0))
    out = pl.pallas_call(
        couple_kernel,
        out_shape=pltpu.HBM(shape, jnp.float32),
        grid=(COLS,),
        in_specs=[SMEM, SMEM, SMEM, spec, spec],
        out_specs=spec,
        scratch_shapes=[pltpu.VMEM((CH, 24, LANES), jnp.float32)],
        compiler_params=params(6),
        cost_estimate=cost(1 << 28, 8 << 20),
        name="couple_terms",
    )(device, coupling, couple, *hbm(field.reshape(shape), image.reshape(shape)))
    return out.reshape(TILES.shape)


def unpack_mirror(recv_ref, mirror, block):
    for y in range(COLS):
        for j in range(3):
            block[...] = recv_ref[pl.ds(y * 3 + j, LANES, stride=EACH), :].T
            for part in range(2):
                for k in range(4):
                    mirror[4 * j + k, pl.ds(row_of(part, y), CH, stride=24), :] = block[
                        pl.ds(part * 4 + k, CH, stride=8), :
                    ]


def live_sums(pair, device_ref, partner_ref, extent_ref, direct_ref, mirror, use):
    here = pl.ds(pl.multiple_of(pair * 48, 16), 48)
    lane, b = position_of(0, device_ref[0])
    for tile in range(COLS):
        rows = []
        for c in range(2):
            channel = pair * 2 + c
            extent = extent_ref[channel]
            there = pl.ds(pl.multiple_of(partner_ref[channel] * 24, 8), 24)
            live = (lane < extent - tile) & (b < extent)
            own = pl.ds(pl.multiple_of(channel * 24, 8), 24)
            total = direct_ref[tile, own, :] + mirror[tile, there, :]
            rows.append(jnp.where(live, total, 0.0))
        use(tile, here, jnp.concatenate(rows, axis=0))


def second_image_kernel(
    device_ref,
    partner_ref,
    extent_ref,
    recv_ref,
    direct_ref,
    op_high_ref,
    op_low_ref,
    field_ref,
    image_ref,
    wire_ref,
    high,
    low,
    mirror,
    block,
    direct,
    field,
    sems,
):
    step = pl.program_id(0)
    fetch = pltpu.make_async_copy(direct_ref, direct, sems.at[0])
    keep = pltpu.make_async_copy(field, field_ref, sems.at[1])

    @pl.when(step == 0)
    def _():
        fetch.start()
        unpack_mirror(recv_ref, mirror, block)
        fetch.wait()

        def use(tile, here, total):
            field[tile, here, :] = total
            lanes = slice(tile * LANES, (tile + 1) * LANES)
            upper = total.astype(jnp.bfloat16)
            high[here, lanes] = upper
            low[here, lanes] = (total - upper.astype(jnp.float32)).astype(jnp.bfloat16)

        @pl.loop(0, CH // 2)
        def _(pair):
            live_sums(pair, device_ref, partner_ref, extent_ref, direct, mirror, use)

        keep.start()

    radial_step(step, high, low, op_high_ref, op_low_ref, image_ref, wire_ref)

    @pl.when(step == COLS // TURN - 1)
    def _():
        keep.wait()


def second_image(device, partner, extent, recv, direct, op_high, op_low):
    return pl.pallas_call(
        second_image_kernel,
        out_shape=(TILES, TILES, SENT),
        grid=(COLS // TURN,),
        in_specs=[SMEM, SMEM, SMEM, VMEM, HBM, OP_SPEC, OP_SPEC],
        out_specs=(HBM, IMAGE_SPEC, SENT_SPEC),
        scratch_shapes=[
            pltpu.VMEM((ROWS, NR), jnp.bfloat16),
            pltpu.VMEM((ROWS, NR), jnp.bfloat16),
            HELD,
            pltpu.VMEM((LANES, LANES), jnp.float32),
            HELD,
            HELD,
            pltpu.SemaphoreType.DMA((2,)),
        ],
        compiler_params=params(36),
        cost_estimate=cost(FLOPS, 25 << 20),
        name="second_image",
    )(device, partner, extent, recv, *hbm(direct, op_high, op_low))


def pack_first_kernel(field_ref, wire_ref):
    for tile in range(COLS):
        for k in range(3):
            block = field_ref[tile, k * LANES : (k + 1) * LANES, :].T
            for s in range(STR):
                start = s * 288 + k * 96 + tile
                wire_ref[pl.ds(start, 8, stride=COLS), :] = block[8 * s : 8 * s + 8, :]


def pack_first(field):
    return pl.pallas_call(
        pack_first_kernel,
        out_shape=SENT,
        grid=(1,),
        in_specs=[TILES_SPEC],
        out_specs=SENT_SPEC,
        compiler_params=params(12),
        cost_estimate=cost(1 << 24, 5 << 20),
        name="pack_first",
    )(*hbm(field))


def place_first_kernel(recv_ref, out_ref, rows):
    for s in range(STR):
        for k in range(3):
            start = s * 288 + k * 96
            block = recv_ref[start : start + 96, :].T
            for i in range(16):
                c, t = divmod(16 * k + i, 3)
                for part in range(2):
                    at = 8 * i + 4 * part
                    rows[part * CH + c, 12 * s + 4 * t : 12 * s + 4 * t + 4, :] = block[
                        at : at + 4, :
                    ]
    for i in range(2 * CH):
        out_ref[i] = rows[i].T


def place_first(recv):
    out = pl.pallas_call(
        place_first_kernel,
        out_shape=jax.ShapeDtypeStruct((2 * CH, 96, 192), jnp.float32),
        grid=(1,),
        in_specs=[SENT_SPEC],
        out_specs=pl.BlockSpec((2 * CH, 96, 192), lambda i: (0, 0, 0)),
        scratch_shapes=[pltpu.VMEM((2 * CH, 192, 96), jnp.float32)],
        compiler_params=params(24),
        cost_estimate=cost(1 << 24, 5 << 20),
        name="place_first",
    )(*hbm(recv))
    return out.reshape(2, CH, 96, 192)


def second_vector_kernel(
    device_ref,
    partner_ref,
    extent_ref,
    recv_ref,
    direct_ref,
    field_ref,
    output_ref,
    mirror,
    result,
    block,
):
    unpack_mirror(recv_ref, mirror, block)

    def keep(tile, here, total):
        result[tile, here, :] = 2.0 * total - field_ref[tile, here, :]

    @pl.loop(0, CH // 2)
    def _(pair):
        live_sums(pair, device_ref, partner_ref, extent_ref, direct_ref, mirror, keep)

    for tile in range(COLS):
        for t in range(3):
            regs = swap_groups(
                result[tile, 24 * c + 8 * t : 24 * c + 8 * t + 8, :] for c in range(CH)
            )
            for s in range(STR):
                start = s * 288 + tile * 24 + t * 8
                output_ref[start : start + 8, :] = regs[s]


def second_vector(device, partner, extent, recv, direct, field):
    return pl.pallas_call(
        second_vector_kernel,
        out_shape=SENT,
        grid=(1,),
        in_specs=[SMEM, SMEM, SMEM, VMEM, TILES_SPEC, TILES_SPEC],
        out_specs=SENT_SPEC,
        scratch_shapes=[HELD, HELD, pltpu.VMEM((LANES, LANES), jnp.float32)],
        compiler_params=params(32),
        cost_estimate=cost(1 << 24, 10 << 20),
        name="second_vector",
    )(device, partner, extent, recv, *hbm(direct, field))


def place_output_kernel(recv_ref, out_ref, rows, left, right):
    part = pl.program_id(0)
    for ya in range(COLS):
        for s in range(STR):
            for t in range(3):
                start = s * 288 + ya * 24 + t * 8
                block = recv_ref[start : start + 8, :]
                block = jnp.where(part == 0, block[:4], block[4:])
                rows[12 * s + 4 * t : 12 * s + 4 * t + 4, :] = block
        turned = rows[...].T
        left[pl.ds(ya, LANES, stride=COLS), :] = turned[:, :LANES]
        right[pl.ds(ya, LANES, stride=COLS), :] = turned[:, LANES:]
    out_ref[0, :, :LANES] = left[...]
    out_ref[0, :, LANES:] = right[:, :64]


def place_output(recv):
    out = pl.pallas_call(
        place_output_kernel,
        out_shape=jax.ShapeDtypeStruct((2, NR, 192), jnp.float32),
        grid=(2,),
        in_specs=[VMEM],
        out_specs=pl.BlockSpec((1, NR, 192), lambda i: (i, 0, 0)),
        scratch_shapes=[
            pltpu.VMEM((256, LANES), jnp.float32),
            pltpu.VMEM((NR, LANES), jnp.float32),
            pltpu.VMEM((NR, LANES), jnp.float32),
        ],
        compiler_params=params(20),
        cost_estimate=cost(1 << 24, 5 << 20),
        name="place_output",
    )(recv)
    return out.reshape(2, CH, 96, 192)


def exchange_all(sent):
    sent = sent.reshape(DEV, 9, 4, LANES)
    recv = lax.all_to_all(sent, ("chan", "strip"), 0, 0, tiled=True)
    return recv.reshape(WIRE, LANES)


def exchange_strip(sent):
    sent = sent.reshape(STR, WIRE // STR, LANES)
    return lax.all_to_all(sent, "strip", 0, 0, tiled=True).reshape(WIRE, LANES)


def local(wave_field, radial_op, coupling, couple, partner, extent):
    device = (lax.axis_index("chan") * STR + lax.axis_index("strip")).reshape(1)
    op_high, op_low = order_operator(radial_op)
    recv = exchange_all(pack_input(wave_field.reshape(ROWS, NR)))
    field, image, sent = first_image(recv, op_high, op_low)
    recv = exchange_all(sent)
    direct = couple_terms(device, coupling, couple, field, image)
    first, image, sent = second_image(
        device, partner, extent, recv, direct, op_high, op_low
    )
    recv = exchange_all(sent)
    direct = couple_terms(device, coupling, couple, first, image)
    first_step = place_first(exchange_strip(pack_first(first)))
    output = second_vector(device, partner, extent, recv, direct, field)
    second_step = place_output(exchange_strip(output))
    return (first_step, second_step)


def solution(mesh):
    placed = (P(None, "chan", "strip", None), P(), P(), P(), P(), P())
    return jax.shard_map(
        local,
        mesh=mesh,
        in_specs=placed,
        out_specs=(P(None, None, "strip", "chan"), P(None, None, "strip", "chan")),
        check_vma=False,
    )
```

time: 250 us -> 224 us (0.90)
  blocking collectives: 38.3 us -> 0 us
  waiting for transfers between devices: 66.3 us -> 99.4 us
  Pallas kernels: 105 us -> 92.1 us
  local copies, waits for them, and re-layouts: 11.3 us -> 0.16 us
  starting transfers between devices: 27 us -> 30.5 us
    all_to_all x1 -> x0, blocking collectives: 38.3 us -> none  [exchange_all(): recv = lax.all_to_all(sent, ('chan', 'strip'), 0, 0, tiled=True)]
    all_to_all x2 -> x3, waiting for transfers between devices: 37.9 us -> 69.1 us  [exchange_all(): recv = lax.all_to_all(sent, ('chan', 'strip'), 0, 0, tiled=True)]
    unnamed x30 -> x10, local copies, waits for them, and re-layouts: 11.3 us -> 0.16 us
    pallas_call x1, Pallas kernels: 19.8 us -> 13 us  [first_image(): pl.pallas_call(first_image_kernel, out_shape=(TILES, TILES, SENT), grid=(...]
    pallas_call x2 -> x1, Pallas kernels: 6.31 us -> 2.31 us  [place_output(): pl.pallas_call(place_output_kernel, out_shape=jax.ShapeDtypeStruct((2, NR...]
    all_to_all x2 -> x3, starting transfers between devices: 17.3 us -> 20.8 us  [exchange_all(): recv = lax.all_to_all(sent, ('chan', 'strip'), 0, 0, tiled=True)]
    pallas_call x4 -> x6, Pallas kernels: 48.2 us -> 48 us  [the longest x2 22.3 us: couple_terms(): pl.pallas_call(couple_kernel, out_shape=pltpu.HBM(shape, jnp.float32), gr...]
  transfers between devices with their start and end apart: 4 -> 5, of which waited for: 4 -> 5; matrix products, arithmetic and copies ran while one was open for 0% -> 0% of each run, Pallas kernels for 21% -> 27%
where the time goes in v2:
time: 224 us; the launch traced here: 223 us
  waiting for transfers between devices  99.4 us (44%)
  Pallas kernels  92.1 us (41%)
  starting transfers between devices  30.5 us (14%)
    all_to_all x3, waiting for transfers between devices, exchange_all(): recv = lax.all_to_all(sent, ('chan', 'strip'), 0, 0, tiled=True)  69.1 us
    all_to_all x2, waiting for transfers between devices, exchange_strip(): return lax.all_to_all(sent, 'strip', 0, 0, tiled=True).reshape(WIRE, LANES)  30.3 us
    pallas_call x2, Pallas kernels, couple_terms(): pl.pallas_call(couple_kernel, out_shape=pltpu.HBM(shape, jnp.float32), gr...  22.3 us
    all_to_all x3, starting transfers between devices, exchange_all(): recv = lax.all_to_all(sent, ('chan', 'strip'), 0, 0, tiled=True)  20.8 us
    pallas_call x1, Pallas kernels, order_operator(): pl.pallas_call(order_operator_kernel, out_shape=(out, out), grid=(2 * COL...  15.3 us
    pallas_call x1, Pallas kernels, second_vector(): pl.pallas_call(second_vector_kernel, out_shape=SENT, grid=(1,), in_specs=...  13.5 us
    pallas_call x1, Pallas kernels, second_image(): pl.pallas_call(second_image_kernel, out_shape=(TILES, TILES, SENT), grid=...  13 us
    pallas_call x1, Pallas kernels, first_image(): pl.pallas_call(first_image_kernel, out_shape=(TILES, TILES, SENT), grid=(...  13 us
  transfers between devices with their start and end apart: 5, of which 5 were waited for; matrix products, arithmetic and copies ran while one was open for 0% of the time, Pallas kernels for 27%

profile of v2, /device:TPU:1, one launch (start us, length us, event | category | flops | bytes accessed | tf_op | source)
XLA Modules:
  0.0 222.9 jit_solution(14909054107504663387)
XLA Ops:
  0.6 3.7 %pack_input.1 = f32[4608,128]{1,0:T(8,128)} custom-call(f32[384,1536]{1,0:T(8,128)} %bitcast.32), custom_call_target="tpu_custom_call" | custom-call | tf_op jit(solution)/shard_map/pack_input/pallas_call | solution.py:76
  4.4 11.5 %all-to-all-start = ((f32[128,9,4,128]{3,2,1,0:T(4,128)}), f32[128,9,4,128]{3,2,1,0:T(4,128)S(1)}, u32[]{:S(2)}, u32[]{:S(2)}) async-start(f32[128,9,4,128]{3,2,1,0:T(4,128)} %bitcast.27), calls=%async_computation | async-start | bytes 4718592 | tf_op jit(solution)/shard_map/all_to_all | solution.py:499
  15.9 15.3 %order_operator.1 = (bf16[12,1536,128]{2,1,0:T(8,128)(2,1)}, bf16[12,1536,128]{2,1,0:T(8,128)(2,1)}) custom-call(f32[1536,1536]{1,0:T(8,128)} %in_ref.1), custom_call_target="tpu_custom_call" | custom-call | flops 16777216 | bytes 18874368 | tf_op jit(solution)/shard_map/order_operator/pallas_call | solution.py:110
  31.2 17.7 %all-to-all-done = f32[128,9,4,128]{3,2,1,0:T(4,128)S(1)} async-done(((f32[128,9,4,128]{3,2,1,0:T(4,128)}), f32[128,9,4,128]{3,2,1,0:T(4,128)S(1)}, u32[]{:S(2)}, u32[]{:S(2)}) %all-to-all-start) | async-done | bytes 2359328 | tf_op jit(solution)/shard_map/all_to_all | solution.py:499
  49.0 13.0 %first_image.1 = (f32[12,384,128]{2,1,0:T(8,128)}, f32[12,384,128]{2,1,0:T(8,128)}, f32[4608,128]{1,0:T(8,128)}) custom-call(f32[4608,128]{1,0:T(8,128)S(1)} %bitcast.23, bf16[12,1536,128]{2,1,0:T(8,128)(2,1)} %get-tuple-element.10.op_high_ref, bf16[12,1536,128]{2,1,0:T(8,128)(2,1)} %get-tuple-element.11.op_low_ref), custom_call_target="tpu_custom_call" | custom-call | flops 5435817984 | bytes 20971520 | tf_op jit(solution)/shard_map/first_image/pallas_call | solution.py:198
  61.9 0.0 copy-start.3
  62.0 0.0 copy-start.2
  62.0 4.6 %all-to-all-start.1 = ((f32[128,9,4,128]{3,2,1,0:T(4,128)}), f32[128,9,4,128]{3,2,1,0:T(4,128)S(1)}, u32[]{:S(2)}, u32[]{:S(2)}) async-start(f32[128,9,4,128]{3,2,1,0:T(4,128)} %bitcast.33), calls=%async_computation.1 | async-start | bytes 4718592 | tf_op jit(solution)/shard_map/all_to_all | solution.py:499
  66.6 0.0 copy-done.3
  66.6 0.1 copy.9.couple_ref
  66.7 0.0 copy-done.2
  66.7 0.1 copy.8.coupling_ref
  66.8 0.0 copy-start
  66.8 0.0 copy-start.1
  66.8 11.2 %couple_terms.2 = f32[12,16,24,128]{3,2,1,0:T(8,128)} custom-call(s32[1]{0:T(128)} %bitcast.device_ref, f32[2,16,8]{2,1,0:T(8,128)S(1)} %copy.8.coupling_ref, s32[16,8]{1,0:T(8,128)S(1)} %copy.9.couple_ref, f32[12,16,24,128]{3,2,1,0:T(8,128)} %bitcast.25, f32[12,16,24,128]{3,2,1,0:T(8,128)} %bitcast.35), custom_call_target="tpu_custom_call" | custom-call | flops 268435456 | bytes 8388608 | tf_op jit(solution)/shard_map/couple_terms/pallas_call | solution.py:252
  77.9 21.9 %all-to-all-done.1 = f32[128,9,4,128]{3,2,1,0:T(4,128)S(1)} async-done(((f32[128,9,4,128]{3,2,1,0:T(4,128)}), f32[128,9,4,128]{3,2,1,0:T(4,128)S(1)}, u32[]{:S(2)}, u32[]{:S(2)}) %all-to-all-start.1) | async-done | bytes 2359328 | tf_op jit(solution)/shard_map/all_to_all | solution.py:499
  99.8 0.0 copy-done
  99.8 0.0 copy-done.1
  99.8 13.0 %second_image.1 = (f32[12,384,128]{2,1,0:T(8,128)}, f32[12,384,128]{2,1,0:T(8,128)}, f32[4608,128]{1,0:T(8,128)}) custom-call(s32[1]{0:T(128)} %bitcast.device_ref, s32[16]{0:T(128)S(1)} %copy-done, s32[16]{0:T(128)S(1)} %copy-done.1, f32[4608,128]{1,0:T(8,128)S(1)} %bitcast.22, f32[12,384,128]{2,1,0:T(8,128)} %bitcast.37, ...), custom_call_target="tpu_custom_call" | custom-call | flops 5435817984 | bytes 26214400 | tf_op jit(solution)/shard_map/second_image/pallas_call | solution.py:343
  112.9 4.6 %all-to-all-start.3 = ((f32[128,9,4,128]{3,2,1,0:T(4,128)}), f32[128,9,4,128]{3,2,1,0:T(4,128)S(1)}, u32[]{:S(2)}, u32[]{:S(2)}) async-start(f32[128,9,4,128]{3,2,1,0:T(4,128)} %bitcast.34), calls=%async_computation.3 | async-start | bytes 4718592 | tf_op jit(solution)/shard_map/all_to_all | solution.py:499
  117.5 3.8 %pack_first.1 = f32[4608,128]{1,0:T(8,128)} custom-call(f32[12,384,128]{2,1,0:T(8,128)} %get-tuple-element.15.field_ref), custom_call_target="tpu_custom_call" | custom-call | flops 16777216 | bytes 5242880 | tf_op jit(solution)/shard_map/pack_first/pallas_call | solution.py:374
  121.3 29.5 %all-to-all-done.3 = f32[128,9,4,128]{3,2,1,0:T(4,128)S(1)} async-done(((f32[128,9,4,128]{3,2,1,0:T(4,128)}), f32[128,9,4,128]{3,2,1,0:T(4,128)S(1)}, u32[]{:S(2)}, u32[]{:S(2)}) %all-to-all-start.3) | async-done | bytes 2359328 | tf_op jit(solution)/shard_map/all_to_all | solution.py:499
  150.8 5.3 %all-to-all-start.2 = ((f32[16,288,128]{2,1,0:T(8,128)}), f32[16,288,128]{2,1,0:T(8,128)}, u32[]{:S(2)}, u32[]{:S(2)}) async-start(f32[16,288,128]{2,1,0:T(8,128)} %bitcast.26), calls=%async_computation.2 | async-start | bytes 4718592 | tf_op jit(solution)/shard_map/all_to_all | solution.py:505
  156.1 11.2 %couple_terms.3 = f32[12,16,24,128]{3,2,1,0:T(8,128)} custom-call(s32[1]{0:T(128)} %bitcast.device_ref, f32[2,16,8]{2,1,0:T(8,128)S(1)} %copy.8.coupling_ref, s32[16,8]{1,0:T(8,128)S(1)} %copy.9.couple_ref, f32[12,16,24,128]{3,2,1,0:T(8,128)} %bitcast.29, f32[12,16,24,128]{3,2,1,0:T(8,128)} %bitcast.36), custom_call_target="tpu_custom_call" | custom-call | flops 268435456 | bytes 8388608 | tf_op jit(solution)/shard_map/couple_terms/pallas_call | solution.py:252
  167.2 13.5 %second_vector.1 = f32[4608,128]{1,0:T(8,128)} custom-call(s32[1]{0:T(128)} %bitcast.device_ref, s32[16]{0:T(128)S(1)} %copy-done, s32[16]{0:T(128)S(1)} %copy-done.1, f32[4608,128]{1,0:T(8,128)S(1)} %bitcast.20, f32[12,384,128]{2,1,0:T(8,128)} %bitcast.28, f32[12,384,128]{2,1,0:T(8,128)} %get-tuple-element.13.field_ref), custom_call_target="tpu_custom_call" | custom-call | flops 16777216 | bytes 10485760 | tf_op jit(solution)/shard_map/second_vector/pallas_call | solution.py:449
  180.7 5.5 %all-to-all-done.2 = f32[16,288,128]{2,1,0:T(8,128)} async-done(((f32[16,288,128]{2,1,0:T(8,128)}), f32[16,288,128]{2,1,0:T(8,128)}, u32[]{:S(2)}, u32[]{:S(2)}) %all-to-all-start.2) | async-done | bytes 2359328 | tf_op jit(solution)/shard_map/all_to_all | solution.py:505
  186.2 4.4 %all-to-all-start.4 = ((f32[16,288,128]{2,1,0:T(8,128)}), f32[16,288,128]{2,1,0:T(8,128)S(1)}, u32[]{:S(2)}, u32[]{:S(2)}) async-start(f32[16,288,128]{2,1,0:T(8,128)} %bitcast.24), calls=%async_computation.4 | async-start | bytes 4718592 | tf_op jit(solution)/shard_map/all_to_all | solution.py:505
  190.6 5.2 %place_first.1 = f32[32,96,192]{2,1,0:T(8,128)} custom-call(f32[4608,128]{1,0:T(8,128)} %bitcast.10.recv_ref), custom_call_target="tpu_custom_call" | custom-call | flops 16777216 | bytes 5242880 | tf_op jit(solution)/shard_map/place_first/pallas_call | solution.py:403
  195.8 24.8 %all-to-all-done.4 = f32[16,288,128]{2,1,0:T(8,128)S(1)} async-done(((f32[16,288,128]{2,1,0:T(8,128)}), f32[16,288,128]{2,1,0:T(8,128)S(1)}, u32[]{:S(2)}, u32[]{:S(2)}) %all-to-all-start.4) | async-done | bytes 2359328 | tf_op jit(solution)/shard_map/all_to_all | solution.py:505
  220.6 2.3 %place_output.1 = f32[2,1536,192]{2,1,0:T(8,128)} custom-call(f32[4608,128]{1,0:T(8,128)S(1)} %bitcast.21), custom_call_target="tpu_custom_call" | custom-call | flops 16777216 | bytes 5242880 | tf_op jit(solution)/shard_map/place_output/pallas_call | solution.py:479
Async XLA Ops:
  4.4 44.6 %all-to-all-start = ((f32[128,9,4,128]{3,2,1,0:T(4,128)}), f32[128,9,4,128]{3,2,1,0:T(4,128)S(1)}, u32[]{:S(2)}, u32[]{:S(2)}) async-start(f32[128,9,4,128]{3,2,1,0:T(4,128)} %bitcast.27), calls=%async_computation | async-start | bytes 4718592 | tf_op jit(solution)/shard_map/all_to_all | solution.py:499
  61.9 4.7 %copy-start.3 = (s32[16,8]{0,1:T(8,128)S(1)}, s32[16,8]{0,1:T(8,128)}, u32[]{:S(2)}) copy-start(s32[16,8]{0,1:T(8,128)} %param.9) | copy-start | bytes 1540
  62.0 4.7 %copy-start.2 = (f32[2,16,8]{1,2,0:T(8,128)S(1)}, f32[2,16,8]{1,2,0:T(8,128)}, u32[]{:S(2)}) copy-start(f32[2,16,8]{1,2,0:T(8,128)} %param.8) | copy-start | bytes 3076
  62.0 37.9 %all-to-all-start.1 = ((f32[128,9,4,128]{3,2,1,0:T(4,128)}), f32[128,9,4,128]{3,2,1,0:T(4,128)S(1)}, u32[]{:S(2)}, u32[]{:S(2)}) async-start(f32[128,9,4,128]{3,2,1,0:T(4,128)} %bitcast.33), calls=%async_computation.1 | async-start | bytes 4718592 | tf_op jit(solution)/shard_map/all_to_all | solution.py:499
  66.8 33.1 %copy-start = (s32[16]{0:T(128)S(1)}, s32[16]{0:T(128)}, u32[]{:S(2)}) copy-start(s32[16]{0:T(128)} %partner_ref.3) | copy-start | bytes 196
  66.8 33.1 %copy-start.1 = (s32[16]{0:T(128)S(1)}, s32[16]{0:T(128)}, u32[]{:S(2)}) copy-start(s32[16]{0:T(128)} %extent_ref.3) | copy-start | bytes 196
  112.9 37.9 %all-to-all-start.3 = ((f32[128,9,4,128]{3,2,1,0:T(4,128)}), f32[128,9,4,128]{3,2,1,0:T(4,128)S(1)}, u32[]{:S(2)}, u32[]{:S(2)}) async-start(f32[128,9,4,128]{3,2,1,0:T(4,128)} %bitcast.34), calls=%async_computation.3 | async-start | bytes 4718592 | tf_op jit(solution)/shard_map/all_to_all | solution.py:499
  150.8 35.4 %all-to-all-start.2 = ((f32[16,288,128]{2,1,0:T(8,128)}), f32[16,288,128]{2,1,0:T(8,128)}, u32[]{:S(2)}, u32[]{:S(2)}) async-start(f32[16,288,128]{2,1,0:T(8,128)} %bitcast.26), calls=%async_computation.2 | async-start | bytes 4718592 | tf_op jit(solution)/shard_map/all_to_all | solution.py:505
  186.2 34.4 %all-to-all-start.4 = ((f32[16,288,128]{2,1,0:T(8,128)}), f32[16,288,128]{2,1,0:T(8,128)S(1)}, u32[]{:S(2)}, u32[]{:S(2)}) async-start(f32[16,288,128]{2,1,0:T(8,128)} %bitcast.24), calls=%async_computation.4 | async-start | bytes 4718592 | tf_op jit(solution)/shard_map/all_to_all | solution.py:505

commit v3 on v2

--- a/solution.py
+++ b/solution.py
@@ -29,8 +29,17 @@
 TILES_SPEC = pl.BlockSpec((COLS, ROWS, LANES), lambda i: (0, 0, 0))
 HELD = pltpu.VMEM((COLS, ROWS, LANES), jnp.float32)
 TURN = 4
-OP_SPEC = pl.BlockSpec((TURN, NR, LANES), lambda i: (i, 0, 0))
-IMAGE_SPEC = pl.BlockSpec((TURN, ROWS, LANES), lambda i: (i, 0, 0))
+TURNS = COLS // TURN
+PRODUCT_SCRATCH = [
+    pltpu.VMEM((ROWS, NR), jnp.bfloat16),
+    pltpu.VMEM((ROWS, NR), jnp.bfloat16),
+    pltpu.VMEM((COLS, NR, LANES), jnp.bfloat16),
+    pltpu.VMEM((COLS, NR, LANES), jnp.bfloat16),
+    HELD,
+    pltpu.VMEM((WIRE, LANES), jnp.float32),
+    pltpu.SemaphoreType.DMA((2 * TURNS,)),
+    pltpu.SemaphoreType.DMA((TURNS + 1,)),
+]
 FLOPS = 2 * 3 * ROWS * NR * NR
 
 
@@ -64,21 +73,42 @@
     return pl.CostEstimate(flops=flops, bytes_accessed=moved, transcendentals=0)
 
 
-def pack_input_kernel(in_ref, out_ref):
-    for tile in range(COLS):
-        lanes = slice(tile * LANES, (tile + 1) * LANES)
-        for j in range(3):
-            block = in_ref[j * LANES : (j + 1) * LANES, lanes]
-            out_ref[pl.ds(tile * ROWS + j, LANES, stride=3), :] = block.T
+def pack_input_kernel(in_ref, out_ref, field, wire, in_sems, out_sems):
+    copies = []
+    for j in range(3):
+        rows = pl.ds(j * LANES, LANES)
+        copies.append(pltpu.make_async_copy(in_ref.at[rows], field.at[rows], in_sems.at[j]))
+        copies[-1].start()
+    out = []
+    for j in range(3):
+        copies[j].wait()
+        for tile in range(COLS):
+            lanes = slice(tile * LANES, (tile + 1) * LANES)
+            block = field[j * LANES : (j + 1) * LANES, lanes]
+            wire[pl.ds(tile * ROWS + j, LANES, stride=3), :] = block.T
+            if j == 2 and tile % 3 == 2:
+                rows = pl.ds((tile - 2) * ROWS, 3 * ROWS)
+                copy = pltpu.make_async_copy(
+                    wire.at[rows], out_ref.at[rows], out_sems.at[tile // 3]
+                )
+                copy.start()
+                out.append(copy)
+    for copy in out:
+        copy.wait()
 
 
 def pack_input(wave):
     return pl.pallas_call(
         pack_input_kernel,
         out_shape=SENT,
-        grid=(1,),
-        in_specs=[pl.BlockSpec((ROWS, NR), lambda i: (0, 0))],
-        out_specs=SENT_SPEC,
+        in_specs=[HBM],
+        out_specs=HBM,
+        scratch_shapes=[
+            pltpu.VMEM((ROWS, NR), jnp.float32),
+            pltpu.VMEM((WIRE, LANES), jnp.float32),
+            pltpu.SemaphoreType.DMA((3,)),
+            pltpu.SemaphoreType.DMA((4,)),
+        ],
         compiler_params=params(12),
         name="pack_input",
     )(*hbm(wave))
@@ -130,19 +160,48 @@
         ).astype(jnp.bfloat16)
 
 
-def radial_step(step, high, low, op_high_ref, op_low_ref, image_ref, wire_ref):
-    op_high = jnp.concatenate([op_high_ref[i] for i in range(TURN)], axis=1)
-    op_low = jnp.concatenate([op_low_ref[i] for i in range(TURN)], axis=1)
-    image = jnp.dot(high[...], op_high, preferred_element_type=jnp.float32)
-    image += jnp.dot(low[...], op_high, preferred_element_type=jnp.float32)
-    image += jnp.dot(high[...], op_low, preferred_element_type=jnp.float32)
-    for i in range(TURN):
-        block = image[:, i * LANES : (i + 1) * LANES]
-        image_ref[i] = block
+def operator_copies(op_high_ref, op_low_ref, op_high, op_low, sems):
+    copies = []
+    for turn in range(TURNS):
+        tiles = pl.ds(turn * TURN, TURN)
+        for k, (src, dst) in enumerate(((op_high_ref, op_high), (op_low_ref, op_low))):
+            copies.append(
+                pltpu.make_async_copy(src.at[tiles], dst.at[tiles], sems.at[2 * turn + k])
+            )
+    return copies
+
+
+def pack_image(tiles, image, wire):
+    for tile in tiles:
         for j in range(3):
-            regs = [block[24 * c + 8 * j : 24 * c + 8 * j + 8, :] for c in range(CH)]
-            start = (step * TURN + i) * 3 + j
-            wire_ref[pl.ds(start, LANES, stride=EACH), :] = jnp.concatenate(regs, axis=0).T
+            regs = [image[tile, 24 * c + 8 * j : 24 * c + 8 * j + 8, :] for c in range(CH)]
+            rows = pl.ds(tile * 3 + j, LANES, stride=EACH)
+            wire[rows, :] = jnp.concatenate(regs, axis=0).T
+
+
+def radial_image(copies, high, low, op_high, op_low, image, image_ref, wire, wire_ref, sems):
+    out = []
+    for turn in range(TURNS):
+        tiles = range(turn * TURN, (turn + 1) * TURN)
+        copies[2 * turn].wait()
+        copies[2 * turn + 1].wait()
+        upper = jnp.concatenate([op_high[i] for i in tiles], axis=1)
+        lower = jnp.concatenate([op_low[i] for i in tiles], axis=1)
+        total = jnp.dot(high[...], upper, preferred_element_type=jnp.float32)
+        total += jnp.dot(low[...], upper, preferred_element_type=jnp.float32)
+        total += jnp.dot(high[...], lower, preferred_element_type=jnp.float32)
+        for i, tile in enumerate(tiles):
+            image[tile] = total[:, i * LANES : (i + 1) * LANES]
+        if turn > 0:
+            pack_image(range((turn - 1) * TURN, turn * TURN), image, wire)
+        part = pl.ds(turn * TURN, TURN)
+        out.append(pltpu.make_async_copy(image.at[part], image_ref.at[part], sems.at[turn]))
+        out[-1].start()
+    pack_image(range((TURNS - 1) * TURN, COLS), image, wire)
+    out.append(pltpu.make_async_copy(wire, wire_ref, sems.at[TURNS]))
+    out[-1].start()
+    for copy in out:
+        copy.wait()
 
 
 def unpack_input(recv_ref, field_ref, held):
@@ -174,41 +233,42 @@
     wire_ref,
     high,
     low,
+    op_high,
+    op_low,
+    image,
+    wire,
+    op_sems,
+    out_sems,
     held,
     field,
     sem,
 ):
-    step = pl.program_id(0)
+    copies = operator_copies(op_high_ref, op_low_ref, op_high, op_low, op_sems)
+    for copy in copies:
+        copy.start()
+    unpack_input(recv_ref, field, held)
     keep = pltpu.make_async_copy(field, field_ref, sem)
-
-    @pl.when(step == 0)
-    def _():
-        unpack_input(recv_ref, field, held)
-        keep.start()
-        split_terms(field, high, low)
-
-    radial_step(step, high, low, op_high_ref, op_low_ref, image_ref, wire_ref)
-
-    @pl.when(step == COLS // TURN - 1)
-    def _():
-        keep.wait()
+    keep.start()
+    split_terms(field, high, low)
+    radial_image(
+        copies, high, low, op_high, op_low, image, image_ref, wire, wire_ref, out_sems
+    )
+    keep.wait()
 
 
 def first_image(recv, op_high, op_low):
     return pl.pallas_call(
         first_image_kernel,
         out_shape=(TILES, TILES, SENT),
-        grid=(COLS // TURN,),
-        in_specs=[VMEM, OP_SPEC, OP_SPEC],
-        out_specs=(HBM, IMAGE_SPEC, SENT_SPEC),
-        scratch_shapes=[
-            pltpu.VMEM((ROWS, NR), jnp.bfloat16),
-            pltpu.VMEM((ROWS, NR), jnp.bfloat16),
+        in_specs=[VMEM, HBM, HBM],
+        out_specs=(HBM, HBM, HBM),
+        scratch_shapes=PRODUCT_SCRATCH
+        + [
             pltpu.VMEM((STR * ROWS, LANES), jnp.float32),
             HELD,
             pltpu.SemaphoreType.DMA,
         ],
-        compiler_params=params(32),
+        compiler_params=params(36),
         cost_estimate=cost(FLOPS, 20 << 20),
         name="first_image",
     )(recv, *hbm(op_high, op_low))
@@ -276,18 +336,19 @@
 
 def live_sums(pair, device_ref, partner_ref, extent_ref, direct_ref, mirror, use):
     here = pl.ds(pl.multiple_of(pair * 48, 16), 48)
-    lane, b = position_of(0, device_ref[0])
+    lane = 12 * lax.broadcasted_iota(jnp.int32, (48, LANES), 1)
+    _, b = position_of(0, device_ref[0])
+    reach, there = [], []
+    for c in range(2):
+        extent = extent_ref[pair * 2 + c]
+        partner = partner_ref[pair * 2 + c]
+        reach.append(jnp.where(b < extent, extent, 0))
+        there.append(pl.ds(pl.multiple_of(partner * 24, 8), 24))
+    reach = jnp.concatenate(reach, axis=0) - lane
     for tile in range(COLS):
-        rows = []
-        for c in range(2):
-            channel = pair * 2 + c
-            extent = extent_ref[channel]
-            there = pl.ds(pl.multiple_of(partner_ref[channel] * 24, 8), 24)
-            live = (lane < extent - tile) & (b < extent)
-            own = pl.ds(pl.multiple_of(channel * 24, 8), 24)
-            total = direct_ref[tile, own, :] + mirror[tile, there, :]
-            rows.append(jnp.where(live, total, 0.0))
-        use(tile, here, jnp.concatenate(rows, axis=0))
+        other = jnp.concatenate([mirror[tile, rows, :] for rows in there], axis=0)
+        total = direct_ref[tile, here, :] + other
+        use(tile, here, jnp.where(reach > tile, total, 0.0))
 
 
 def second_image_kernel(
@@ -303,52 +364,53 @@
     wire_ref,
     high,
     low,
+    op_high,
+    op_low,
+    image,
+    wire,
+    op_sems,
+    out_sems,
     mirror,
     block,
     direct,
     field,
     sems,
 ):
-    step = pl.program_id(0)
     fetch = pltpu.make_async_copy(direct_ref, direct, sems.at[0])
+    fetch.start()
+    copies = operator_copies(op_high_ref, op_low_ref, op_high, op_low, op_sems)
+    for copy in copies:
+        copy.start()
+    unpack_mirror(recv_ref, mirror, block)
+    fetch.wait()
+
+    def use(tile, here, total):
+        field[tile, here, :] = total
+        lanes = slice(tile * LANES, (tile + 1) * LANES)
+        upper = total.astype(jnp.bfloat16)
+        high[here, lanes] = upper
+        low[here, lanes] = (total - upper.astype(jnp.float32)).astype(jnp.bfloat16)
+
+    @pl.loop(0, CH // 2)
+    def _(pair):
+        live_sums(pair, device_ref, partner_ref, extent_ref, direct, mirror, use)
+
     keep = pltpu.make_async_copy(field, field_ref, sems.at[1])
-
-    @pl.when(step == 0)
-    def _():
-        fetch.start()
-        unpack_mirror(recv_ref, mirror, block)
-        fetch.wait()
-
-        def use(tile, here, total):
-            field[tile, here, :] = total
-            lanes = slice(tile * LANES, (tile + 1) * LANES)
-            upper = total.astype(jnp.bfloat16)
-            high[here, lanes] = upper
-            low[here, lanes] = (total - upper.astype(jnp.float32)).astype(jnp.bfloat16)
-
-        @pl.loop(0, CH // 2)
-        def _(pair):
-            live_sums(pair, device_ref, partner_ref, extent_ref, direct, mirror, use)
-
-        keep.start()
-
-    radial_step(step, high, low, op_high_ref, op_low_ref, image_ref, wire_ref)
-
-    @pl.when(step == COLS // TURN - 1)
-    def _():
-        keep.wait()
+    keep.start()
+    radial_image(
+        copies, high, low, op_high, op_low, image, image_ref, wire, wire_ref, out_sems
+    )
+    keep.wait()
 
 
 def second_image(device, partner, extent, recv, direct, op_high, op_low):
     return pl.pallas_call(
         second_image_kernel,
         out_shape=(TILES, TILES, SENT),
-        grid=(COLS // TURN,),
-        in_specs=[SMEM, SMEM, SMEM, VMEM, HBM, OP_SPEC, OP_SPEC],
-        out_specs=(HBM, IMAGE_SPEC, SENT_SPEC),
-        scratch_shapes=[
-            pltpu.VMEM((ROWS, NR), jnp.bfloat16),
-            pltpu.VMEM((ROWS, NR), jnp.bfloat16),
+        in_specs=[SMEM, SMEM, SMEM, VMEM, HBM, HBM, HBM],
+        out_specs=(HBM, HBM, HBM),
+        scratch_shapes=PRODUCT_SCRATCH
+        + [
             HELD,
             pltpu.VMEM((LANES, LANES), jnp.float32),
             HELD,

time: 224 us -> 220 us (0.982)
  Pallas kernels: 92.1 us -> 87.7 us
    pallas_call x3, Pallas kernels: 29.7 us -> 25.5 us  [the longest x1 11.2 us: second_image(): pl.pallas_call(second_image_kernel, out_shape=(TILES, TILES, SENT), in_sp...]
where the time goes in v3:
time: 220 us; the launch traced here: 219 us
  waiting for transfers between devices  99.5 us (45%)
  Pallas kernels  87.7 us (40%)
  starting transfers between devices  30.5 us (14%)
    all_to_all x3, waiting for transfers between devices, exchange_all(): recv = lax.all_to_all(sent, ('chan', 'strip'), 0, 0, tiled=True)  69.1 us
    all_to_all x2, waiting for transfers between devices, exchange_strip(): return lax.all_to_all(sent, 'strip', 0, 0, tiled=True).reshape(WIRE, LANES)  30.4 us
    pallas_call x2, Pallas kernels, couple_terms(): pl.pallas_call(couple_kernel, out_shape=pltpu.HBM(shape, jnp.float32), gr...  22.3 us
    all_to_all x3, starting transfers between devices, exchange_all(): recv = lax.all_to_all(sent, ('chan', 'strip'), 0, 0, tiled=True)  20.8 us
    pallas_call x1, Pallas kernels, order_operator(): pl.pallas_call(order_operator_kernel, out_shape=(out, out), grid=(2 * COL...  15.3 us
    pallas_call x1, Pallas kernels, second_vector(): pl.pallas_call(second_vector_kernel, out_shape=SENT, grid=(1,), in_specs=...  13.4 us
    pallas_call x1, Pallas kernels, second_image(): pl.pallas_call(second_image_kernel, out_shape=(TILES, TILES, SENT), in_sp...  11.2 us
    pallas_call x1, Pallas kernels, first_image(): pl.pallas_call(first_image_kernel, out_shape=(TILES, TILES, SENT), in_spe...  11 us
  transfers between devices with their start and end apart: 5, of which 5 were waited for; matrix products, arithmetic and copies ran while one was open for 0% of the time, Pallas kernels for 27%

profile of v3, /device:TPU:1, one launch (start us, length us, event | category | flops | bytes accessed | tf_op | source)
XLA Modules:
  0.0 218.6 jit_solution(10180172275129857902)
XLA Ops:
  0.6 3.3 %pack_input.1 = f32[4608,128]{1,0:T(8,128)} custom-call(f32[384,1536]{1,0:T(8,128)} %bitcast.32), custom_call_target="tpu_custom_call" | custom-call | tf_op jit(solution)/shard_map/pack_input/pallas_call | solution.py:101
  3.9 11.5 %all-to-all-start = ((f32[128,9,4,128]{3,2,1,0:T(4,128)}), f32[128,9,4,128]{3,2,1,0:T(4,128)S(1)}, u32[]{:S(2)}, u32[]{:S(2)}) async-start(f32[128,9,4,128]{3,2,1,0:T(4,128)} %bitcast.27), calls=%async_computation | async-start | bytes 4718592 | tf_op jit(solution)/shard_map/all_to_all | solution.py:561
  15.4 15.3 %order_operator.1 = (bf16[12,1536,128]{2,1,0:T(8,128)(2,1)}, bf16[12,1536,128]{2,1,0:T(8,128)(2,1)}) custom-call(f32[1536,1536]{1,0:T(8,128)} %in_ref.1), custom_call_target="tpu_custom_call" | custom-call | flops 16777216 | bytes 18874368 | tf_op jit(solution)/shard_map/order_operator/pallas_call | solution.py:140
  30.8 17.7 %all-to-all-done = f32[128,9,4,128]{3,2,1,0:T(4,128)S(1)} async-done(((f32[128,9,4,128]{3,2,1,0:T(4,128)}), f32[128,9,4,128]{3,2,1,0:T(4,128)S(1)}, u32[]{:S(2)}, u32[]{:S(2)}) %all-to-all-start) | async-done | bytes 2359328 | tf_op jit(solution)/shard_map/all_to_all | solution.py:561
  48.5 11.0 %first_image.1 = (f32[12,384,128]{2,1,0:T(8,128)}, f32[12,384,128]{2,1,0:T(8,128)}, f32[4608,128]{1,0:T(8,128)}) custom-call(f32[4608,128]{1,0:T(8,128)S(1)} %bitcast.23, bf16[12,1536,128]{2,1,0:T(8,128)(2,1)} %get-tuple-element.10.op_high_ref, bf16[12,1536,128]{2,1,0:T(8,128)(2,1)} %get-tuple-element.11.op_low_ref), custom_call_target="tpu_custom_call" | custom-call | flops 5435817984 | bytes 20971520 | tf_op jit(solution)/shard_map/first_image/pallas_call | solution.py:260
  59.5 0.0 copy-start.3
  59.5 0.0 copy-start.2
  59.5 4.6 %all-to-all-start.1 = ((f32[128,9,4,128]{3,2,1,0:T(4,128)}), f32[128,9,4,128]{3,2,1,0:T(4,128)S(1)}, u32[]{:S(2)}, u32[]{:S(2)}) async-start(f32[128,9,4,128]{3,2,1,0:T(4,128)} %bitcast.33), calls=%async_computation.1 | async-start | bytes 4718592 | tf_op jit(solution)/shard_map/all_to_all | solution.py:561
  64.1 0.0 copy-done.3
  64.2 0.1 copy.9.couple_ref
  64.2 0.0 copy-done.2
  64.2 0.1 copy.8.coupling_ref
  64.3 0.0 copy-start
  64.3 0.0 copy-start.1
  64.3 11.2 %couple_terms.2 = f32[12,16,24,128]{3,2,1,0:T(8,128)} custom-call(s32[1]{0:T(128)} %bitcast.device_ref, f32[2,16,8]{2,1,0:T(8,128)S(1)} %copy.8.coupling_ref, s32[16,8]{1,0:T(8,128)S(1)} %copy.9.couple_ref, f32[12,16,24,128]{3,2,1,0:T(8,128)} %bitcast.25, f32[12,16,24,128]{3,2,1,0:T(8,128)} %bitcast.35), custom_call_target="tpu_custom_call" | custom-call | flops 268435456 | bytes 8388608 | tf_op jit(solution)/shard_map/couple_terms/pallas_call | solution.py:312
  75.5 21.9 %all-to-all-done.1 = f32[128,9,4,128]{3,2,1,0:T(4,128)S(1)} async-done(((f32[128,9,4,128]{3,2,1,0:T(4,128)}), f32[128,9,4,128]{3,2,1,0:T(4,128)S(1)}, u32[]{:S(2)}, u32[]{:S(2)}) %all-to-all-start.1) | async-done | bytes 2359328 | tf_op jit(solution)/shard_map/all_to_all | solution.py:561
  97.4 0.0 copy-done
  97.4 0.0 copy-done.1
  97.4 11.2 %second_image.1 = (f32[12,384,128]{2,1,0:T(8,128)}, f32[12,384,128]{2,1,0:T(8,128)}, f32[4608,128]{1,0:T(8,128)}) custom-call(s32[1]{0:T(128)} %bitcast.device_ref, s32[16]{0:T(128)S(1)} %copy-done, s32[16]{0:T(128)S(1)} %copy-done.1, f32[4608,128]{1,0:T(8,128)S(1)} %bitcast.22, f32[12,384,128]{2,1,0:T(8,128)} %bitcast.37, ...), custom_call_target="tpu_custom_call" | custom-call | flops 5435817984 | bytes 26214400 | tf_op jit(solution)/shard_map/second_image/pallas_call | solution.py:407
  108.6 4.6 %all-to-all-start.3 = ((f32[128,9,4,128]{3,2,1,0:T(4,128)}), f32[128,9,4,128]{3,2,1,0:T(4,128)S(1)}, u32[]{:S(2)}, u32[]{:S(2)}) async-start(f32[128,9,4,128]{3,2,1,0:T(4,128)} %bitcast.34), calls=%async_computation.3 | async-start | bytes 4718592 | tf_op jit(solution)/shard_map/all_to_all | solution.py:561
  113.3 3.8 %pack_first.1 = f32[4608,128]{1,0:T(8,128)} custom-call(f32[12,384,128]{2,1,0:T(8,128)} %get-tuple-element.15.field_ref), custom_call_target="tpu_custom_call" | custom-call | flops 16777216 | bytes 5242880 | tf_op jit(solution)/shard_map/pack_first/pallas_call | solution.py:436
  117.0 29.5 %all-to-all-done.3 = f32[128,9,4,128]{3,2,1,0:T(4,128)S(1)} async-done(((f32[128,9,4,128]{3,2,1,0:T(4,128)}), f32[128,9,4,128]{3,2,1,0:T(4,128)S(1)}, u32[]{:S(2)}, u32[]{:S(2)}) %all-to-all-start.3) | async-done | bytes 2359328 | tf_op jit(solution)/shard_map/all_to_all | solution.py:561
  146.5 5.3 %all-to-all-start.2 = ((f32[16,288,128]{2,1,0:T(8,128)}), f32[16,288,128]{2,1,0:T(8,128)}, u32[]{:S(2)}, u32[]{:S(2)}) async-start(f32[16,288,128]{2,1,0:T(8,128)} %bitcast.26), calls=%async_computation.2 | async-start | bytes 4718592 | tf_op jit(solution)/shard_map/all_to_all | solution.py:567
  151.8 11.1 %couple_terms.3 = f32[12,16,24,128]{3,2,1,0:T(8,128)} custom-call(s32[1]{0:T(128)} %bitcast.device_ref, f32[2,16,8]{2,1,0:T(8,128)S(1)} %copy.8.coupling_ref, s32[16,8]{1,0:T(8,128)S(1)} %copy.9.couple_ref, f32[12,16,24,128]{3,2,1,0:T(8,128)} %bitcast.29, f32[12,16,24,128]{3,2,1,0:T(8,128)} %bitcast.36), custom_call_target="tpu_custom_call" | custom-call | flops 268435456 | bytes 8388608 | tf_op jit(solution)/shard_map/couple_terms/pallas_call | solution.py:312
  163.0 13.4 %second_vector.1 = f32[4608,128]{1,0:T(8,128)} custom-call(s32[1]{0:T(128)} %bitcast.device_ref, s32[16]{0:T(128)S(1)} %copy-done, s32[16]{0:T(128)S(1)} %copy-done.1, f32[4608,128]{1,0:T(8,128)S(1)} %bitcast.20, f32[12,384,128]{2,1,0:T(8,128)} %bitcast.28, f32[12,384,128]{2,1,0:T(8,128)} %get-tuple-element.13.field_ref), custom_call_target="tpu_custom_call" | custom-call | flops 16777216 | bytes 10485760 | tf_op jit(solution)/shard_map/second_vector/pallas_call | solution.py:511
  176.3 5.6 %all-to-all-done.2 = f32[16,288,128]{2,1,0:T(8,128)} async-done(((f32[16,288,128]{2,1,0:T(8,128)}), f32[16,288,128]{2,1,0:T(8,128)}, u32[]{:S(2)}, u32[]{:S(2)}) %all-to-all-start.2) | async-done | bytes 2359328 | tf_op jit(solution)/shard_map/all_to_all | solution.py:567
  181.9 4.4 %all-to-all-start.4 = ((f32[16,288,128]{2,1,0:T(8,128)}), f32[16,288,128]{2,1,0:T(8,128)S(1)}, u32[]{:S(2)}, u32[]{:S(2)}) async-start(f32[16,288,128]{2,1,0:T(8,128)} %bitcast.24), calls=%async_computation.4 | async-start | bytes 4718592 | tf_op jit(solution)/shard_map/all_to_all | solution.py:567
  186.3 5.2 %place_first.1 = f32[32,96,192]{2,1,0:T(8,128)} custom-call(f32[4608,128]{1,0:T(8,128)} %bitcast.10.recv_ref), custom_call_target="tpu_custom_call" | custom-call | flops 16777216 | bytes 5242880 | tf_op jit(solution)/shard_map/place_first/pallas_call | solution.py:465
  191.5 24.8 %all-to-all-done.4 = f32[16,288,128]{2,1,0:T(8,128)S(1)} async-done(((f32[16,288,128]{2,1,0:T(8,128)}), f32[16,288,128]{2,1,0:T(8,128)S(1)}, u32[]{:S(2)}, u32[]{:S(2)}) %all-to-all-start.4) | async-done | bytes 2359328 | tf_op jit(solution)/shard_map/all_to_all | solution.py:567
  216.3 2.3 %place_output.1 = f32[2,1536,192]{2,1,0:T(8,128)} custom-call(f32[4608,128]{1,0:T(8,128)S(1)} %bitcast.21), custom_call_target="tpu_custom_call" | custom-call | flops 16777216 | bytes 5242880 | tf_op jit(solution)/shard_map/place_output/pallas_call | solution.py:541
Async XLA Ops:
  3.9 44.6 %all-to-all-start = ((f32[128,9,4,128]{3,2,1,0:T(4,128)}), f32[128,9,4,128]{3,2,1,0:T(4,128)S(1)}, u32[]{:S(2)}, u32[]{:S(2)}) async-start(f32[128,9,4,128]{3,2,1,0:T(4,128)} %bitcast.27), calls=%async_computation | async-start | bytes 4718592 | tf_op jit(solution)/shard_map/all_to_all | solution.py:561
  59.5 4.7 %copy-start.3 = (s32[16,8]{0,1:T(8,128)S(1)}, s32[16,8]{0,1:T(8,128)}, u32[]{:S(2)}) copy-start(s32[16,8]{0,1:T(8,128)} %param.9) | copy-start | bytes 1540
  59.5 4.8 %copy-start.2 = (f32[2,16,8]{1,2,0:T(8,128)S(1)}, f32[2,16,8]{1,2,0:T(8,128)}, u32[]{:S(2)}) copy-start(f32[2,16,8]{1,2,0:T(8,128)} %param.8) | copy-start | bytes 3076
  59.5 37.9 %all-to-all-start.1 = ((f32[128,9,4,128]{3,2,1,0:T(4,128)}), f32[128,9,4,128]{3,2,1,0:T(4,128)S(1)}, u32[]{:S(2)}, u32[]{:S(2)}) async-start(f32[128,9,4,128]{3,2,1,0:T(4,128)} %bitcast.33), calls=%async_computation.1 | async-start | bytes 4718592 | tf_op jit(solution)/shard_map/all_to_all | solution.py:561
  64.3 33.1 %copy-start = (s32[16]{0:T(128)S(1)}, s32[16]{0:T(128)}, u32[]{:S(2)}) copy-start(s32[16]{0:T(128)} %partner_ref.3) | copy-start | bytes 196
  64.3 33.1 %copy-start.1 = (s32[16]{0:T(128)S(1)}, s32[16]{0:T(128)}, u32[]{:S(2)}) copy-start(s32[16]{0:T(128)} %extent_ref.3) | copy-start | bytes 196
  108.6 37.9 %all-to-all-start.3 = ((f32[128,9,4,128]{3,2,1,0:T(4,128)}), f32[128,9,4,128]{3,2,1,0:T(4,128)S(1)}, u32[]{:S(2)}, u32[]{:S(2)}) async-start(f32[128,9,4,128]{3,2,1,0:T(4,128)} %bitcast.34), calls=%async_computation.3 | async-start | bytes 4718592 | tf_op jit(solution)/shard_map/all_to_all | solution.py:561
  146.5 35.4 %all-to-all-start.2 = ((f32[16,288,128]{2,1,0:T(8,128)}), f32[16,288,128]{2,1,0:T(8,128)}, u32[]{:S(2)}, u32[]{:S(2)}) async-start(f32[16,288,128]{2,1,0:T(8,128)} %bitcast.26), calls=%async_computation.2 | async-start | bytes 4718592 | tf_op jit(solution)/shard_map/all_to_all | solution.py:567
  181.9 34.4 %all-to-all-start.4 = ((f32[16,288,128]{2,1,0:T(8,128)}), f32[16,288,128]{2,1,0:T(8,128)S(1)}, u32[]{:S(2)}, u32[]{:S(2)}) async-start(f32[16,288,128]{2,1,0:T(8,128)} %bitcast.24), calls=%async_computation.4 | async-start | bytes 4718592 | tf_op jit(solution)/shard_map/all_to_all | solution.py:567

commit v4 on v3

--- a/solution.py
+++ b/solution.py
@@ -75,24 +75,23 @@
 
 def pack_input_kernel(in_ref, out_ref, field, wire, in_sems, out_sems):
     copies = []
-    for j in range(3):
-        rows = pl.ds(j * LANES, LANES)
-        copies.append(pltpu.make_async_copy(in_ref.at[rows], field.at[rows], in_sems.at[j]))
+    for k in range(4):
+        part = pl.ds(k * 3 * LANES, 3 * LANES)
+        copies.append(
+            pltpu.make_async_copy(in_ref.at[:, part], field.at[:, part], in_sems.at[k])
+        )
         copies[-1].start()
     out = []
-    for j in range(3):
-        copies[j].wait()
-        for tile in range(COLS):
-            lanes = slice(tile * LANES, (tile + 1) * LANES)
-            block = field[j * LANES : (j + 1) * LANES, lanes]
-            wire[pl.ds(tile * ROWS + j, LANES, stride=3), :] = block.T
-            if j == 2 and tile % 3 == 2:
-                rows = pl.ds((tile - 2) * ROWS, 3 * ROWS)
-                copy = pltpu.make_async_copy(
-                    wire.at[rows], out_ref.at[rows], out_sems.at[tile // 3]
-                )
-                copy.start()
-                out.append(copy)
+    for k in range(4):
+        copies[k].wait()
+        for tile in range(3 * k, 3 * k + 3):
+            for j in range(3):
+                lanes = slice(tile * LANES, (tile + 1) * LANES)
+                block = field[j * LANES : (j + 1) * LANES, lanes]
+                wire[pl.ds(tile * ROWS + j, LANES, stride=3), :] = block.T
+        rows = pl.ds(k * 3 * ROWS, 3 * ROWS)
+        out.append(pltpu.make_async_copy(wire.at[rows], out_ref.at[rows], out_sems.at[k]))
+        out[-1].start()
     for copy in out:
         copy.wait()
 
@@ -106,7 +105,7 @@
         scratch_shapes=[
             pltpu.VMEM((ROWS, NR), jnp.float32),
             pltpu.VMEM((WIRE, LANES), jnp.float32),
-            pltpu.SemaphoreType.DMA((3,)),
+            pltpu.SemaphoreType.DMA((4,)),
             pltpu.SemaphoreType.DMA((4,)),
         ],
         compiler_params=params(12),
@@ -150,14 +149,11 @@
     )(*hbm(radial_op))
 
 
-def split_terms(tiles_ref, high, low):
-    for tile in range(COLS):
-        block = tiles_ref[tile]
-        upper = block.astype(jnp.bfloat16)
-        high[:, tile * LANES : (tile + 1) * LANES] = upper
-        low[:, tile * LANES : (tile + 1) * LANES] = (
-            block - upper.astype(jnp.float32)
-        ).astype(jnp.bfloat16)
+def split_terms(block, tile, rows, high, low):
+    lanes = slice(tile * LANES, (tile + 1) * LANES)
+    upper = block.astype(jnp.bfloat16)
+    high[rows, lanes] = upper
+    low[rows, lanes] = (block - upper.astype(jnp.float32)).astype(jnp.bfloat16)
 
 
 def operator_copies(op_high_ref, op_low_ref, op_high, op_low, sems):
@@ -204,7 +200,7 @@
         copy.wait()
 
 
-def unpack_input(recv_ref, field_ref, held):
+def unpack_input(recv_ref, field_ref, held, high, low):
     for s in range(STR):
         for j in range(3):
             rows = [
@@ -213,8 +209,8 @@
             ]
             start = s * ROWS + j * LANES
             held[start : start + LANES, :96] = jnp.concatenate(rows, axis=0).T
-    for pc in range(4):
-        for ya in range(COLS):
+    for ya in range(COLS):
+        for pc in range(4):
             rows = [
                 held[pl.ds(s * ROWS + pc * 96 + ya, 8, stride=COLS), :] for s in range(STR)
             ]
@@ -222,6 +218,7 @@
             for y in range(COLS):
                 start = (pc % 2) * 24 + row_of(pc // 2, y)
                 field_ref[ya, pl.ds(start, 8, stride=48), :] = block[8 * y : 8 * y + 8, :]
+        split_terms(field_ref[ya], ya, slice(0, ROWS), high, low)
 
 
 def first_image_kernel(
@@ -246,10 +243,9 @@
     copies = operator_copies(op_high_ref, op_low_ref, op_high, op_low, op_sems)
     for copy in copies:
         copy.start()
-    unpack_input(recv_ref, field, held)
+    unpack_input(recv_ref, field, held, high, low)
     keep = pltpu.make_async_copy(field, field_ref, sem)
     keep.start()
-    split_terms(field, high, low)
     radial_image(
         copies, high, low, op_high, op_low, image, image_ref, wire, wire_ref, out_sems
     )
@@ -386,10 +382,7 @@
 
     def use(tile, here, total):
         field[tile, here, :] = total
-        lanes = slice(tile * LANES, (tile + 1) * LANES)
-        upper = total.astype(jnp.bfloat16)
-        high[here, lanes] = upper
-        low[here, lanes] = (total - upper.astype(jnp.float32)).astype(jnp.bfloat16)
+        split_terms(total, tile, here, high, low)
 
     @pl.loop(0, CH // 2)
     def _(pair):

time: 220 us -> 220 us (level)
  no operation moved by 1% of the time
where the time goes in v4:
time: 220 us; the launch traced here: 218 us
  waiting for transfers between devices  99.5 us (45%)
  Pallas kernels  87.4 us (40%)
  starting transfers between devices  30.5 us (14%)
    all_to_all x3, waiting for transfers between devices, exchange_all(): recv = lax.all_to_all(sent, ('chan', 'strip'), 0, 0, tiled=True)  69.1 us
    all_to_all x2, waiting for transfers between devices, exchange_strip(): return lax.all_to_all(sent, 'strip', 0, 0, tiled=True).reshape(WIRE, LANES)  30.4 us
    pallas_call x2, Pallas kernels, couple_terms(): pl.pallas_call(couple_kernel, out_shape=pltpu.HBM(shape, jnp.float32), gr...  22.3 us
    all_to_all x3, starting transfers between devices, exchange_all(): recv = lax.all_to_all(sent, ('chan', 'strip'), 0, 0, tiled=True)  20.8 us
    pallas_call x1, Pallas kernels, order_operator(): pl.pallas_call(order_operator_kernel, out_shape=(out, out), grid=(2 * COL...  15.3 us
    pallas_call x1, Pallas kernels, second_vector(): pl.pallas_call(second_vector_kernel, out_shape=SENT, grid=(1,), in_specs=...  13.4 us
    pallas_call x1, Pallas kernels, second_image(): pl.pallas_call(second_image_kernel, out_shape=(TILES, TILES, SENT), in_sp...  11.2 us
    pallas_call x1, Pallas kernels, first_image(): pl.pallas_call(first_image_kernel, out_shape=(TILES, TILES, SENT), in_spe...  11 us
  transfers between devices with their start and end apart: 5, of which 5 were waited for; matrix products, arithmetic and copies ran while one was open for 0% of the time, Pallas kernels for 27%

profile of v4, /device:TPU:1, one launch (start us, length us, event | category | flops | bytes accessed | tf_op | source)
XLA Modules:
  0.0 218.3 jit_solution(15954280527771182877)
XLA Ops:
  0.6 2.9 %pack_input.1 = f32[4608,128]{1,0:T(8,128)} custom-call(f32[384,1536]{1,0:T(8,128)} %bitcast.32), custom_call_target="tpu_custom_call" | custom-call | tf_op jit(solution)/shard_map/pack_input/pallas_call | solution.py:100
  3.5 11.5 %all-to-all-start = ((f32[128,9,4,128]{3,2,1,0:T(4,128)}), f32[128,9,4,128]{3,2,1,0:T(4,128)S(1)}, u32[]{:S(2)}, u32[]{:S(2)}) async-start(f32[128,9,4,128]{3,2,1,0:T(4,128)} %bitcast.27), calls=%async_computation | async-start | bytes 4718592 | tf_op jit(solution)/shard_map/all_to_all | solution.py:554
  15.0 15.3 %order_operator.1 = (bf16[12,1536,128]{2,1,0:T(8,128)(2,1)}, bf16[12,1536,128]{2,1,0:T(8,128)(2,1)}) custom-call(f32[1536,1536]{1,0:T(8,128)} %in_ref.1), custom_call_target="tpu_custom_call" | custom-call | flops 16777216 | bytes 18874368 | tf_op jit(solution)/shard_map/order_operator/pallas_call | solution.py:139
  30.4 17.7 %all-to-all-done = f32[128,9,4,128]{3,2,1,0:T(4,128)S(1)} async-done(((f32[128,9,4,128]{3,2,1,0:T(4,128)}), f32[128,9,4,128]{3,2,1,0:T(4,128)S(1)}, u32[]{:S(2)}, u32[]{:S(2)}) %all-to-all-start) | async-done | bytes 2359328 | tf_op jit(solution)/shard_map/all_to_all | solution.py:554
  48.1 11.0 %first_image.1 = (f32[12,384,128]{2,1,0:T(8,128)}, f32[12,384,128]{2,1,0:T(8,128)}, f32[4608,128]{1,0:T(8,128)}) custom-call(f32[4608,128]{1,0:T(8,128)S(1)} %bitcast.23, bf16[12,1536,128]{2,1,0:T(8,128)(2,1)} %get-tuple-element.10.op_high_ref, bf16[12,1536,128]{2,1,0:T(8,128)(2,1)} %get-tuple-element.11.op_low_ref), custom_call_target="tpu_custom_call" | custom-call | flops 5435817984 | bytes 20971520 | tf_op jit(solution)/shard_map/first_image/pallas_call | solution.py:256
  59.1 0.0 copy-start.3
  59.1 0.0 copy-start.2
  59.1 4.6 %all-to-all-start.1 = ((f32[128,9,4,128]{3,2,1,0:T(4,128)}), f32[128,9,4,128]{3,2,1,0:T(4,128)S(1)}, u32[]{:S(2)}, u32[]{:S(2)}) async-start(f32[128,9,4,128]{3,2,1,0:T(4,128)} %bitcast.33), calls=%async_computation.1 | async-start | bytes 4718592 | tf_op jit(solution)/shard_map/all_to_all | solution.py:554
  63.8 0.0 copy-done.3
  63.8 0.1 copy.9.couple_ref
  63.9 0.0 copy-done.2
  63.9 0.1 copy.8.coupling_ref
  63.9 0.0 copy-start
  63.9 0.0 copy-start.1
  63.9 11.2 %couple_terms.2 = f32[12,16,24,128]{3,2,1,0:T(8,128)} custom-call(s32[1]{0:T(128)} %bitcast.device_ref, f32[2,16,8]{2,1,0:T(8,128)S(1)} %copy.8.coupling_ref, s32[16,8]{1,0:T(8,128)S(1)} %copy.9.couple_ref, f32[12,16,24,128]{3,2,1,0:T(8,128)} %bitcast.25, f32[12,16,24,128]{3,2,1,0:T(8,128)} %bitcast.35), custom_call_target="tpu_custom_call" | custom-call | flops 268435456 | bytes 8388608 | tf_op jit(solution)/shard_map/couple_terms/pallas_call | solution.py:308
  75.1 21.9 %all-to-all-done.1 = f32[128,9,4,128]{3,2,1,0:T(4,128)S(1)} async-done(((f32[128,9,4,128]{3,2,1,0:T(4,128)}), f32[128,9,4,128]{3,2,1,0:T(4,128)S(1)}, u32[]{:S(2)}, u32[]{:S(2)}) %all-to-all-start.1) | async-done | bytes 2359328 | tf_op jit(solution)/shard_map/all_to_all | solution.py:554
  97.0 0.0 copy-done
  97.0 0.0 copy-done.1
  97.0 11.2 %second_image.1 = (f32[12,384,128]{2,1,0:T(8,128)}, f32[12,384,128]{2,1,0:T(8,128)}, f32[4608,128]{1,0:T(8,128)}) custom-call(s32[1]{0:T(128)} %bitcast.device_ref, s32[16]{0:T(128)S(1)} %copy-done, s32[16]{0:T(128)S(1)} %copy-done.1, f32[4608,128]{1,0:T(8,128)S(1)} %bitcast.22, f32[12,384,128]{2,1,0:T(8,128)} %bitcast.37, ...), custom_call_target="tpu_custom_call" | custom-call | flops 5435817984 | bytes 26214400 | tf_op jit(solution)/shard_map/second_image/pallas_call | solution.py:400
  108.2 4.6 %all-to-all-start.3 = ((f32[128,9,4,128]{3,2,1,0:T(4,128)}), f32[128,9,4,128]{3,2,1,0:T(4,128)S(1)}, u32[]{:S(2)}, u32[]{:S(2)}) async-start(f32[128,9,4,128]{3,2,1,0:T(4,128)} %bitcast.34), calls=%async_computation.3 | async-start | bytes 4718592 | tf_op jit(solution)/shard_map/all_to_all | solution.py:554
  112.9 3.8 %pack_first.1 = f32[4608,128]{1,0:T(8,128)} custom-call(f32[12,384,128]{2,1,0:T(8,128)} %get-tuple-element.15.field_ref), custom_call_target="tpu_custom_call" | custom-call | flops 16777216 | bytes 5242880 | tf_op jit(solution)/shard_map/pack_first/pallas_call | solution.py:429
  116.7 29.5 %all-to-all-done.3 = f32[128,9,4,128]{3,2,1,0:T(4,128)S(1)} async-done(((f32[128,9,4,128]{3,2,1,0:T(4,128)}), f32[128,9,4,128]{3,2,1,0:T(4,128)S(1)}, u32[]{:S(2)}, u32[]{:S(2)}) %all-to-all-start.3) | async-done | bytes 2359328 | tf_op jit(solution)/shard_map/all_to_all | solution.py:554
  146.1 5.3 %all-to-all-start.2 = ((f32[16,288,128]{2,1,0:T(8,128)}), f32[16,288,128]{2,1,0:T(8,128)}, u32[]{:S(2)}, u32[]{:S(2)}) async-start(f32[16,288,128]{2,1,0:T(8,128)} %bitcast.26), calls=%async_computation.2 | async-start | bytes 4718592 | tf_op jit(solution)/shard_map/all_to_all | solution.py:560
  151.4 11.1 %couple_terms.3 = f32[12,16,24,128]{3,2,1,0:T(8,128)} custom-call(s32[1]{0:T(128)} %bitcast.device_ref, f32[2,16,8]{2,1,0:T(8,128)S(1)} %copy.8.coupling_ref, s32[16,8]{1,0:T(8,128)S(1)} %copy.9.couple_ref, f32[12,16,24,128]{3,2,1,0:T(8,128)} %bitcast.29, f32[12,16,24,128]{3,2,1,0:T(8,128)} %bitcast.36), custom_call_target="tpu_custom_call" | custom-call | flops 268435456 | bytes 8388608 | tf_op jit(solution)/shard_map/couple_terms/pallas_call | solution.py:308
  162.6 13.4 %second_vector.1 = f32[4608,128]{1,0:T(8,128)} custom-call(s32[1]{0:T(128)} %bitcast.device_ref, s32[16]{0:T(128)S(1)} %copy-done, s32[16]{0:T(128)S(1)} %copy-done.1, f32[4608,128]{1,0:T(8,128)S(1)} %bitcast.20, f32[12,384,128]{2,1,0:T(8,128)} %bitcast.28, f32[12,384,128]{2,1,0:T(8,128)} %get-tuple-element.13.field_ref), custom_call_target="tpu_custom_call" | custom-call | flops 16777216 | bytes 10485760 | tf_op jit(solution)/shard_map/second_vector/pallas_call | solution.py:504
  176.0 5.6 %all-to-all-done.2 = f32[16,288,128]{2,1,0:T(8,128)} async-done(((f32[16,288,128]{2,1,0:T(8,128)}), f32[16,288,128]{2,1,0:T(8,128)}, u32[]{:S(2)}, u32[]{:S(2)}) %all-to-all-start.2) | async-done | bytes 2359328 | tf_op jit(solution)/shard_map/all_to_all | solution.py:560
  181.6 4.4 %all-to-all-start.4 = ((f32[16,288,128]{2,1,0:T(8,128)}), f32[16,288,128]{2,1,0:T(8,128)S(1)}, u32[]{:S(2)}, u32[]{:S(2)}) async-start(f32[16,288,128]{2,1,0:T(8,128)} %bitcast.24), calls=%async_computation.4 | async-start | bytes 4718592 | tf_op jit(solution)/shard_map/all_to_all | solution.py:560
  185.9 5.2 %place_first.1 = f32[32,96,192]{2,1,0:T(8,128)} custom-call(f32[4608,128]{1,0:T(8,128)} %bitcast.10.recv_ref), custom_call_target="tpu_custom_call" | custom-call | flops 16777216 | bytes 5242880 | tf_op jit(solution)/shard_map/place_first/pallas_call | solution.py:458
  191.1 24.8 %all-to-all-done.4 = f32[16,288,128]{2,1,0:T(8,128)S(1)} async-done(((f32[16,288,128]{2,1,0:T(8,128)}), f32[16,288,128]{2,1,0:T(8,128)S(1)}, u32[]{:S(2)}, u32[]{:S(2)}) %all-to-all-start.4) | async-done | bytes 2359328 | tf_op jit(solution)/shard_map/all_to_all | solution.py:560
  216.0 2.3 %place_output.1 = f32[2,1536,192]{2,1,0:T(8,128)} custom-call(f32[4608,128]{1,0:T(8,128)S(1)} %bitcast.21), custom_call_target="tpu_custom_call" | custom-call | flops 16777216 | bytes 5242880 | tf_op jit(solution)/shard_map/place_output/pallas_call | solution.py:534
Async XLA Ops:
  3.5 44.6 %all-to-all-start = ((f32[128,9,4,128]{3,2,1,0:T(4,128)}), f32[128,9,4,128]{3,2,1,0:T(4,128)S(1)}, u32[]{:S(2)}, u32[]{:S(2)}) async-start(f32[128,9,4,128]{3,2,1,0:T(4,128)} %bitcast.27), calls=%async_computation | async-start | bytes 4718592 | tf_op jit(solution)/shard_map/all_to_all | solution.py:554
  59.1 4.7 %copy-start.3 = (s32[16,8]{0,1:T(8,128)S(1)}, s32[16,8]{0,1:T(8,128)}, u32[]{:S(2)}) copy-start(s32[16,8]{0,1:T(8,128)} %param.9) | copy-start | bytes 1540
  59.1 4.7 %copy-start.2 = (f32[2,16,8]{1,2,0:T(8,128)S(1)}, f32[2,16,8]{1,2,0:T(8,128)}, u32[]{:S(2)}) copy-start(f32[2,16,8]{1,2,0:T(8,128)} %param.8) | copy-start | bytes 3076
  59.1 37.9 %all-to-all-start.1 = ((f32[128,9,4,128]{3,2,1,0:T(4,128)}), f32[128,9,4,128]{3,2,1,0:T(4,128)S(1)}, u32[]{:S(2)}, u32[]{:S(2)}) async-start(f32[128,9,4,128]{3,2,1,0:T(4,128)} %bitcast.33), calls=%async_computation.1 | async-start | bytes 4718592 | tf_op jit(solution)/shard_map/all_to_all | solution.py:554
  63.9 33.1 %copy-start = (s32[16]{0:T(128)S(1)}, s32[16]{0:T(128)}, u32[]{:S(2)}) copy-start(s32[16]{0:T(128)} %partner_ref.3) | copy-start | bytes 196
  63.9 33.1 %copy-start.1 = (s32[16]{0:T(128)S(1)}, s32[16]{0:T(128)}, u32[]{:S(2)}) copy-start(s32[16]{0:T(128)} %extent_ref.3) | copy-start | bytes 196
  108.2 37.9 %all-to-all-start.3 = ((f32[128,9,4,128]{3,2,1,0:T(4,128)}), f32[128,9,4,128]{3,2,1,0:T(4,128)S(1)}, u32[]{:S(2)}, u32[]{:S(2)}) async-start(f32[128,9,4,128]{3,2,1,0:T(4,128)} %bitcast.34), calls=%async_computation.3 | async-start | bytes 4718592 | tf_op jit(solution)/shard_map/all_to_all | solution.py:554
  146.1 35.4 %all-to-all-start.2 = ((f32[16,288,128]{2,1,0:T(8,128)}), f32[16,288,128]{2,1,0:T(8,128)}, u32[]{:S(2)}, u32[]{:S(2)}) async-start(f32[16,288,128]{2,1,0:T(8,128)} %bitcast.26), calls=%async_computation.2 | async-start | bytes 4718592 | tf_op jit(solution)/shard_map/all_to_all | solution.py:560
  181.6 34.4 %all-to-all-start.4 = ((f32[16,288,128]{2,1,0:T(8,128)}), f32[16,288,128]{2,1,0:T(8,128)S(1)}, u32[]{:S(2)}, u32[]{:S(2)}) async-start(f32[16,288,128]{2,1,0:T(8,128)} %bitcast.24), calls=%async_computation.4 | async-start | bytes 4718592 | tf_op jit(solution)/shard_map/all_to_all | solution.py:560
